TPU v7x, 32 devices: a whole 2x2x4 slice. The times are simulated.
32 devices in a mesh: seq: 8 (over z, y), chan: 4 (over x, core).
Axes of the slice: x: 2, y: 2, z: 4, core: 2. Of those that a mesh axis runs over, the one named last changes fastest.
Arguments:
- features: bfloat16 [2048, 3, 8192], P(('seq', 'chan')), may hold values from -6 to 6
- cotangent: bfloat16 [2048, 8192], P('seq', 'chan'), may hold values from -6 to 6
- short_filter: float32 [3, 512, 7], P(None, 'chan'), may hold values from -2.5 to 2.5
- medium_filter: float32 [512, 128], P('chan'), may hold values from -0.5 to 0.5
- doc_start: int32 [8], replicated, may hold values from 0 to 255
Outputs:
- hyena_out: bfloat16 [2048, 8192], P('seq', 'chan')
- feature_grad: bfloat16 [2048, 3, 8192], P(('seq', 'chan'))
Inputs may be any that keep to these rules, and one draw needn't show every extreme that they name: Each shard holds exactly one document start, at position doc_start[i] of its 256 positions.
All inputs are finite; a program needn't handle non-finite values.
Results may differ from a plain program's by a relative error of at most 0.006.
Values may be sent and summed in bfloat16 or wider, within the bound.
A program may use at most 128 MiB of HBM per device.

v0:
```python
import jax
import jax.numpy as jnp
from jax import lax
from jax.sharding import PartitionSpec as P

SHORT = 7
MEDIUM = 128


band_rows = 256


def from_behind(block, axis, distance):
    devices = range(lax.axis_size(axis))
    route = [(i - distance, i) for i in devices if i - distance in devices]
    return lax.ppermute(block, axis, route)


def segment_ids(positions, doc_start, shard_rows):
    bounds = jnp.arange(doc_start.shape[0], dtype=jnp.int32) * shard_rows + doc_start
    return jnp.sum((bounds[None, :] <= positions[:, None]).astype(jnp.int32), axis=1)


def short_forward(source, seg_ids, taps_full):
    row_count = source.shape[1] - (SHORT - 1)
    running = jnp.zeros((source.shape[0], row_count, source.shape[2]), jnp.float32)
    for offset in range(SHORT):
        row_start = SHORT - 1 - offset
        shifted = source[:, row_start : row_start + row_count]
        open_tap = seg_ids[row_start : row_start + row_count] == seg_ids[SHORT - 1 :]
        running = running + jnp.where(
            open_tap[None, :, None], taps_full[:, offset, :][:, None, :] * shifted, 0.0
        )
    return running


def short_backward(grad_short, seg_ids, taps_full):
    row_count = grad_short.shape[1]
    out_rows = row_count + SHORT - 1
    grad_padded = jnp.pad(grad_short, ((0, 0), (SHORT - 1, SHORT - 1), (0, 0)))
    seg_padded = jnp.concatenate([seg_ids, jnp.full((SHORT - 1,), -1, jnp.int32)])
    running = jnp.zeros((grad_short.shape[0], out_rows, grad_short.shape[2]), jnp.float32)
    for offset in range(SHORT):
        shifted = grad_padded[:, offset : offset + out_rows]
        open_tap = seg_ids == seg_padded[offset : offset + out_rows]
        running = running + jnp.where(
            open_tap[None, :, None], taps_full[:, offset, :][:, None, :] * shifted, 0.0
        )
    return running


def band_mats(filters_bf, seg_ids):
    lag_steps = (
        jnp.arange(band_rows, dtype=jnp.int32)[:, None]
        + MEDIUM
        - jnp.arange(band_rows + MEDIUM, dtype=jnp.int32)[None, :]
    )
    inside = (lag_steps >= 0) & (lag_steps < MEDIUM)
    lag_table = jnp.where(
        inside[None],
        jnp.take(filters_bf, jnp.clip(lag_steps, 0, MEDIUM - 1), axis=1),
        jnp.zeros((), filters_bf.dtype),
    )
    target_ids = seg_ids[MEDIUM : band_rows + MEDIUM]
    same_doc = target_ids[:, None] == seg_ids[None, :]
    matrices = [jnp.where(same_doc[None], lag_table, jnp.zeros((), lag_table.dtype))]
    return jnp.stack(matrices)


def body(features, cotangent, short_filter, medium_filter, doc_start):
    regrouped = lax.all_to_all(
        jnp.transpose(features, (1, 0, 2)), "chan", split_axis=2, concat_axis=1, tiled=True
    )
    shard_rows = regrouped.shape[1]
    local_width = regrouped.shape[2]
    local_groups = short_filter.shape[1]
    group_width = local_width // local_groups
    rim_reach = MEDIUM + SHORT - 1
    row_base = lax.axis_index("seq") * shard_rows
    positions = row_base - rim_reach + jnp.arange(shard_rows + rim_reach, dtype=jnp.int32)
    seg_all = segment_ids(positions, doc_start, shard_rows)
    taps_full = jnp.repeat(jnp.transpose(short_filter, (0, 2, 1)), group_width, axis=2)
    filters_bf = medium_filter.astype(jnp.bfloat16)
    before = from_behind(regrouped[:, shard_rows - rim_reach :], "seq", 1)
    extended = jnp.concatenate([before, regrouped], axis=1)
    short_ext = short_forward(extended, seg_all, taps_full)
    gated_ext = (short_ext[1] * short_ext[2]).astype(jnp.bfloat16)
    short_own = short_ext[:, MEDIUM:]
    blocks = shard_rows // band_rows
    window_rows = band_rows + MEDIUM
    matrices = band_mats(filters_bf, seg_all[SHORT - 1 :])
    windows = jnp.stack([gated_ext])
    windows = jnp.transpose(
        windows.reshape(blocks, window_rows, local_groups, group_width), (0, 2, 3, 1)
    )
    long_chan = jnp.einsum("bgts,bgcs->bgct", matrices, windows, preferred_element_type=jnp.float32)
    long_conv = jnp.transpose(long_chan, (0, 3, 1, 2)).reshape(shard_rows, local_width)
    query_short = short_own[0]
    key_short = short_own[1]
    value_short = short_own[2]
    hyena_out = (query_short * long_conv).astype(jnp.bfloat16)
    grad_query = cotangent * long_conv
    grad_long = (cotangent * query_short).astype(jnp.bfloat16)
    long_blocks = jnp.transpose(
        grad_long.reshape(blocks, band_rows, local_groups, group_width), (0, 2, 3, 1)
    )
    spread = jnp.einsum(
        "bgts,bgct->bgcs", matrices, long_blocks, preferred_element_type=jnp.float32
    )
    spread = jnp.transpose(spread, (0, 3, 1, 2)).reshape(blocks, window_rows, local_width)
    gated_grad = jnp.zeros((shard_rows + MEDIUM, local_width), jnp.float32)
    gated_grad = gated_grad.at[0:window_rows].add(spread[0])
    own_grad = gated_grad[MEDIUM:]
    seg_back = seg_all[MEDIUM:]
    head_grad = jnp.stack(
        [
            grad_query[: SHORT - 1],
            own_grad[: SHORT - 1] * value_short[: SHORT - 1],
            own_grad[: SHORT - 1] * key_short[: SHORT - 1],
        ],
        axis=0,
    )
    head_spread = short_backward(head_grad, seg_back[: 2 * (SHORT - 1)], taps_full)
    backward_out = jnp.concatenate(
        [gated_grad[:MEDIUM], head_spread[:, : SHORT - 1].reshape(3 * (SHORT - 1), local_width)],
        axis=0,
    )
    backward_in = from_behind(backward_out, "seq", -1)
    own_grad = own_grad.at[shard_rows - MEDIUM :].add(backward_in[:MEDIUM])
    grad_short = jnp.stack([grad_query, own_grad * value_short, own_grad * key_short], axis=0)
    spread_short = short_backward(grad_short, seg_back, taps_full)
    feature_full = (
        spread_short[:, SHORT - 1 :]
        .at[:, shard_rows - SHORT + 1 :]
        .add(backward_in[MEDIUM:].reshape(3, SHORT - 1, local_width))
    )
    restored = lax.all_to_all(
        feature_full.astype(jnp.bfloat16), "chan", split_axis=1, concat_axis=2, tiled=True
    )
    return (hyena_out, jnp.transpose(restored, (1, 0, 2)))


def solution(mesh):
    in_specs = (
        P(("seq", "chan"), None, None),
        P("seq", "chan"),
        P(None, "chan", None),
        P("chan", None),
        P(),
    )
    out_specs = (P("seq", "chan"), P(("seq", "chan"), None, None))
    return jax.shard_map(body, mesh=mesh, in_specs=in_specs, out_specs=out_specs, check_vma=False)
```

profile of v0, /device:TPU:0, one launch (start us, length us, event | category | flops | bytes accessed | tf_op | source)
XLA Modules:
  0.0 708.2 jit_solution(11230173101609217157)
XLA Ops:
  0.6 11.3 %copy.69 = bf16[64,3,8192]{0,1,2:T(4,128)(2,1)} copy(bf16[64,3,8192]{2,0,1:T(8,128)(2,1)} %param.13) | data formatting | bytes 6291456 | tf_op args[0]
  11.9 8.2 %bitcast_bitcast_fusion = bf16[8192,3,64]{2,1,0:T(4,128)(2,1)} fusion(bf16[64,3,8192]{0,1,2:T(4,128)(2,1)} %copy.69), kind=kLoop, calls=%fused_computation.145 | loop fusion | bytes 6291456
  20.1 8.6 %reshape.297 = bf16[4,2,196608]{2,1,0:T(2,128)(2,1)} reshape(bf16[8192,3,64]{2,1,0:T(4,128)(2,1)} %bitcast_bitcast_fusion) | data formatting | bytes 6291456
  28.7 4.2 all-to-all-start
  41.4 28.5 %all-to-all-done = bf16[4,2,196608]{2,1,0:T(2,128)(2,1)S(1)} async-done(((bf16[4,2,196608]{2,1,0:T(2,128)(2,1)}), bf16[4,2,196608]{2,1,0:T(2,128)(2,1)S(1)}, u32[]{:S(2)}, u32[]{:S(2)}) %all-to-all-start) | async-done | bytes 3145760 | tf_op jit(solution)/shard_map/all_to_all | solution.py:71
  69.9 6.4 reshape.298
  76.4 10.7 %copy.71 = bf16[3,4,64,2048]{3,2,1,0:T(8,128)(2,1)S(1)} copy(bf16[3,4,64,2048]{2,0,3,1:T(4,128)(2,1)} %bitcast.101) | data formatting | bytes 6291456 | tf_op jit(solution)/shard_map/all_to_all | solution.py:71
  88.6 5.4 collective-permute-start
  95.0 372.1 %gather_fusion = bf16[98304,128]{1,0:T(8,128)(2,1)} fusion(bf16[128,128]{0,1:T(8,128)(2,1)S(1)} %copy.73, s32[98304]{0:T(1024)} %broadcast_clamp_fusion), kind=kCustom, calls=%fused_computation | custom fusion | bytes 50724864 | tf_op jit(solution)/shard_map/jit(_take)/gather | solution.py:61
  467.1 32.0 %copy.74 = bf16[256,384,128]{1,0,2:T(8,128)(2,1)} copy(bf16[256,384,128]{2,1,0:T(8,128)(2,1)} %bitcast.100) | data formatting | bytes 50331648 | tf_op jit(solution)/shard_map/jit(_take)/gather | solution.py:61
  500.4 44.8 %select_add_fusion = f32[3,384,2048]{2,1,0:T(8,128)S(1)} fusion(bf16[3,256,2048]{2,1,0:T(8,128)(2,1)S(1)} %bitcast.103, bf16[3,134,2048]{2,1,0:T(8,128)(2,1)} %collective-permute-done, f32[3,2048]{1,0:T(4,128)S(1)} %get-tuple-element.91, f32[3,2048]{1,0:T(4,128)S(1)} %get-tuple-element.92, f32[3,2048]{1,0:T(4,128)S(1)} %get-tuple-element.93, ...), kind=kLoop, calls=%fused_computation.18 | loop fusion | flops 110886912 | bytes 14403840 | tf_op jit(solution)/shard_map/add | solution.py:31
  545.2 3.5 copy-done
  550.1 12.9 %fusion.2 = f32[128,16,256]{2,1,0:T(8,128)} fusion(bf16[128,16,384]{2,1,0:T(8,128)(2,1)S(1)} %bitcast.112, bf16[256,384,128]{1,0,2:T(8,128)(2,1)} %copy.74, pred[256,384]{1,0:T(8,128)(4,1)} %get-tuple-element.97, pred[256,384]{1,0:T(8,128)(4,1)} %get-tuple-element.84, pred[256,384]{1,0:T(8,128)(4,1)S(1)} %get-tuple-element.83), kind=kOutput, calls=%fused_computation.3 | convolution fusion | flops 440401920 | bytes 29130752 | tf_op jit(solution)/shard_map/bgts,bgcs->bgct/dot_general | solution.py:96
  564.9 3.8 convert_multiply_fusion.1
  570.2 16.5 %fusion.33 = f32[1,384,128,16]{1,3,2,0:T(8,128)} fusion(bf16[128,16,256]{2,1,0:T(8,128)(2,1)} %bitcast.113, bf16[256,384,128]{1,0,2:T(8,128)(2,1)} %copy.74, pred[256,384]{1,0:T(8,128)(4,1)S(1)} %get-tuple-element.83, pred[256,384]{1,0:T(8,128)(4,1)} %get-tuple-element.84, pred[256,384]{1,0:T(8,128)(4,1)} %get-tuple-element.97), kind=kOutput, calls=%fused_computation.67 | convolution fusion | flops 440401920 | bytes 29655040 | tf_op jit(solution)/shard_map/bgts,bgct->bgcs/dot_general | solution.py:107
  586.7 3.1 fusion.58
  597.4 3.1 slice.397
  600.5 3.1 copy.82
  605.2 21.6 %collective-permute-done.1 = f32[146,2048]{1,0:T(8,128)} collective-permute-done((f32[146,2048]{1,0:T(8,128)}, f32[146,2048]{1,0:T(8,128)}, u32[]{:S(2)}, u32[]{:S(2)}) %collective-permute-start.1) | collective-permute-done | bytes 1196064 | tf_op jit(solution)/shard_map/ppermute | solution.py:16
  629.1 5.4 fusion.32
  636.1 8.0 %fusion.10 = f32[3,262,2048]{2,1,0:T(8,128)S(1)} fusion(f32[3,268,2048]{2,1,0:T(8,128)S(1)} %select_maximum_fusion, f32[3,2048]{1,0:T(4,128)S(1)} %get-tuple-element.91, f32[3,2048]{1,0:T(4,128)S(1)} %get-tuple-element.92, f32[3,2048]{1,0:T(4,128)S(1)} %get-tuple-element.93, f32[3,2048]{1,0:T(4,128)S(1)} %copy-done.4, f32[3,2048]{1,0:T(4,128)S(1)} %get-tuple-element.95, ...), kind=kLoop, calls=%fused_computation.24 | loop fusion | flops 30584832 | bytes 51684900 | tf_op jit(solution)/shard_map/add | solution.py:46
  644.1 2.7 copy-done.1
  650.0 2.7 copy.83
  652.7 50.7 %all_to_all.36 = bf16[3,256,2048]{2,0,1:T(4,128)(2,1)S(1)} all-to-all(bf16[3,256,2048]{2,0,1:T(4,128)(2,1)S(1)} %copy.83), channel_id=1, replica_groups=mesh['seq'=8,'chan'=4] {'chan'}, dimensions={1} | all-to-all | bytes 6291456 | tf_op jit(solution)/shard_map/all_to_all | solution.py:137
  (103 shorter events, 37.0 us)
Async XLA Ops:
  20.0 12.9 %copy-start.26 = (s32[8]{0:T(128)S(1)}, s32[8]{0:T(128)}, u32[]{:S(2)}) copy-start(s32[8]{0:T(128)} %param.17) | copy-start | bytes 100
  20.1 14.1 %copy-start.15 = (f32[3,128,7]{1,2,0:T(8,128)S(1)}, f32[3,128,7]{1,2,0:T(8,128)}, u32[]{:S(2)}) copy-start(f32[3,128,7]{1,2,0:T(8,128)} %param.15) | copy-start | bytes 32260
  28.7 41.2 %all-to-all-start = ((bf16[4,2,196608]{2,1,0:T(2,128)(2,1)}), bf16[4,2,196608]{2,1,0:T(2,128)(2,1)S(1)}, u32[]{:S(2)}, u32[]{:S(2)}) async-start(bf16[4,2,196608]{2,1,0:T(2,128)(2,1)} %reshape.297), calls=%async_computation | async-start | bytes 6291456 | tf_op jit(solution)/shard_map/all_to_all | solution.py:71
  33.0 61.8 %copy-start.5 = (s32[390]{0:T(512)}, s32[390]{0:T(512)S(1)}, u32[]{:S(2)}) copy-start(s32[390]{0:T(512)S(1)} %convert_reduce_fusion) | copy-start | bytes 4684
  76.3 17.7 %copy-start.25 = (s32[12]{0:T(128)S(1)}, s32[12]{0:T(128)}, u32[]{:S(2)}) copy-start(s32[12]{0:T(128)} %slice.338) | copy-start | bytes 148
  76.3 18.5 %copy-start.13 = (f32[3,1,2048]{2,1,0:T(1,128)S(1)}, f32[3,1,2048]{2,1,0:T(1,128)}, u32[]{:S(2)}) copy-start(f32[3,1,2048]{2,1,0:T(1,128)} %get-tuple-element.64) | copy-start | bytes 73732
  76.4 18.5 %copy-start.14 = (f32[128,128]{1,0:T(8,128)S(1)}, f32[128,128]{1,0:T(8,128)}, u32[]{:S(2)}) copy-start(f32[128,128]{1,0:T(8,128)} %param.16) | copy-start | bytes 196612
  88.6 411.7 %collective-permute-start = (bf16[3,134,2048]{2,1,0:T(8,128)(2,1)}, bf16[3,134,2048]{2,1,0:T(8,128)(2,1)}, u32[]{:S(2)}, u32[]{:S(2)}) collective-permute-start(bf16[3,134,2048]{2,1,0:T(8,128)(2,1)} %slice.375), channel_id=1, source_target_pairs={{0,4},{4,8},{8,12},{12,16},{16,20},{20,24},{24,28},{1,5},{5,9},{9,... | collective-permute-start | bytes 4939784 | tf_op jit(solution)/shard_map/ppermute | solution.py:16
  467.1 33.1 %copy-start.11 = (f32[3,1,2048]{2,1,0:T(1,128)S(1)}, f32[3,1,2048]{2,1,0:T(1,128)}, u32[]{:S(2)}) copy-start(f32[3,1,2048]{2,1,0:T(1,128)} %get-tuple-element.65) | copy-start | bytes 73732
  467.1 33.1 %copy-start.12 = (f32[3,1,2048]{2,1,0:T(1,128)S(1)}, f32[3,1,2048]{2,1,0:T(1,128)}, u32[]{:S(2)}) copy-start(f32[3,1,2048]{2,1,0:T(1,128)} %get-tuple-element.66) | copy-start | bytes 73732
  467.1 33.1 %copy-start.9 = (f32[3,1,2048]{2,1,0:T(1,128)S(1)}, f32[3,1,2048]{2,1,0:T(1,128)}, u32[]{:S(2)}) copy-start(f32[3,1,2048]{2,1,0:T(1,128)} %get-tuple-element.67) | copy-start | bytes 73732
  467.1 33.2 %copy-start.10 = (f32[3,1,2048]{2,1,0:T(1,128)S(1)}, f32[3,1,2048]{2,1,0:T(1,128)}, u32[]{:S(2)}) copy-start(f32[3,1,2048]{2,1,0:T(1,128)} %get-tuple-element.68) | copy-start | bytes 73732
  467.1 33.2 %copy-start.7 = (f32[3,1,2048]{2,1,0:T(1,128)S(1)}, f32[3,1,2048]{2,1,0:T(1,128)}, u32[]{:S(2)}) copy-start(f32[3,1,2048]{2,1,0:T(1,128)} %get-tuple-element.69) | copy-start | bytes 73732
  467.1 33.2 %copy-start.8 = (f32[3,1,2048]{2,1,0:T(1,128)S(1)}, f32[3,1,2048]{2,1,0:T(1,128)}, u32[]{:S(2)}) copy-start(f32[3,1,2048]{2,1,0:T(1,128)} %get-tuple-element.70) | copy-start | bytes 73732
  467.1 33.2 %copy-start.22 = (pred[384]{0:T(512)(128)(4,1)S(1)}, pred[384]{0:T(512)(128)(4,1)}, u32[]{:S(2)}) copy-start(pred[384]{0:T(512)(128)(4,1)} %get-tuple-element.79) | copy-start | bytes 1156
  467.1 33.2 %copy-start.23 = (pred[384]{0:T(512)(128)(4,1)S(1)}, pred[384]{0:T(512)(128)(4,1)}, u32[]{:S(2)}) copy-start(pred[384]{0:T(512)(128)(4,1)} %get-tuple-element.80) | copy-start | bytes 1156
  467.1 33.2 %copy-start.24 = (pred[384]{0:T(512)(128)(4,1)S(1)}, pred[384]{0:T(512)(128)(4,1)}, u32[]{:S(2)}) copy-start(pred[384]{0:T(512)(128)(4,1)} %get-tuple-element.81) | copy-start | bytes 1156
  500.3 92.7 %copy-start.3 = (f32[3,2048]{1,0:T(4,128)}, f32[3,2048]{1,0:T(4,128)S(1)}, u32[]{:S(2)}) copy-start(f32[3,2048]{1,0:T(4,128)S(1)} %get-tuple-element.94) | copy-start | bytes 73732
  586.7 6.3 copy-start.16
  586.7 6.3 copy-start.17
  586.7 6.3 copy-start.18
  586.7 6.3 copy-start.19
  586.7 6.3 copy-start.20
  596.0 30.8 %collective-permute-start.1 = (f32[146,2048]{1,0:T(8,128)}, f32[146,2048]{1,0:T(8,128)}, u32[]{:S(2)}, u32[]{:S(2)}) collective-permute-start(f32[146,2048]{1,0:T(8,128)} %pad_maximum_fusion.1), channel_id=1, source_target_pairs={{4,0},{8,4},{12,8},{16,12},{20,16},{24,20},{28,24},{5,1},{9,5},{13... | collective-permute-start | bytes 3588104 | tf_op jit(solution)/shard_map/ppermute | solution.py:16
  (7 other events, 27.0 us)
where the time goes:
time: 722 us; the launch traced here: 708 us
  local copies, waits for them, and re-layouts  491 us (68%)
  other arithmetic  74.1 us (10%)
  blocking collectives  50.7 us (7%)
  waiting for transfers between devices  50.2 us (7%)
  matrix products  29.4 us (4%)
  starting transfers between devices  10.9 us (2%)
    gather x2, local copies, waits for them, and re-layouts, band_mats(): jnp.take(filters_bf, jnp.clip(lag_steps, 0, MEDIUM - 1), axis=1)  404 us
    all_to_all x1, blocking collectives, body(): lax.all_to_all(feature_full.astype(jnp.bfloat16), 'chan', split_axis=1, c...  50.7 us
    add x1, other arithmetic, short_forward(): running + jnp.where(open_tap[None, :, None], taps_full[:, offset, :][:, N...  44.8 us
    unnamed x63, local copies, waits for them, and re-layouts  41.1 us
    all_to_all x1, waiting for transfers between devices, body(): lax.all_to_all(jnp.transpose(features, (1, 0, 2)), 'chan', split_axis=2,...  28.5 us
    ppermute x2, waiting for transfers between devices, from_behind(): return lax.ppermute(block, axis, route)  21.6 us
    dot_general x1, matrix products, body(): jnp.einsum('bgts,bgct->bgcs', matrices, long_blocks, preferred_element_ty...  16.5 us
  transfers between devices with their start and end apart: 3, of which 2 were waited for; matrix products, arithmetic and copies ran while one was open for 60% of the time, Pallas kernels for 0%

commit v1 on v0

v1 whole, which is shorter than its diff:
```python
import functools

import jax
import jax.numpy as jnp
from jax import lax
from jax.experimental import pallas as pl
from jax.experimental.pallas import tpu as pltpu
from jax.sharding import PartitionSpec as P

SHORT = 7
MEDIUM = 128
PAD = 144
TAIL = 16
LANES = 128
MESH = pl.DeviceIdType.MESH
ANY = pl.BlockSpec(memory_space=pl.ANY)


def greet(chans, seqs):
    c, s = lax.axis_index("chan"), lax.axis_index("seq")
    bar = pltpu.get_barrier_semaphore()
    for k in range(1, chans):
        pl.semaphore_signal(bar, inc=1, device_id={"chan": lax.rem(c + k, chans)}, device_id_type=MESH)
    count = chans - 1
    if seqs:
        for k in (1, seqs - 1):
            pl.semaphore_signal(bar, inc=1, device_id={"seq": lax.rem(s + k, seqs)}, device_id_type=MESH)
        count += 2
    pl.semaphore_wait(bar, count)


def gather_kernel(chans, seqs, x, cot, zero, ext, cext, ssem, rsem, lsem, hs, hr):
    c, s = lax.axis_index("chan"), lax.axis_index("seq")
    rows = x.shape[1]
    width = ext.shape[2]
    own = rows * chans
    greet(chans, seqs)

    def block(dst):
        return x.at[:, :, pl.ds(pl.multiple_of(dst * width, width), width)]

    def place(src):
        return ext.at[:, pl.ds(pl.multiple_of(PAD + src * rows, 16), rows), :]

    copies = []
    for k in range(1, chans):
        d = lax.rem(c + k, chans)
        cp = pltpu.make_async_remote_copy(
            block(d), place(c), ssem.at[k], rsem.at[k], device_id={"chan": d}, device_id_type=MESH)
        cp.start()
        copies.append(cp)
    local = [
        pltpu.make_async_copy(block(c), place(c), lsem.at[0]),
        pltpu.make_async_copy(cot, cext.at[pl.ds(0, own)], lsem.at[1]),
    ]
    for cp in local:
        cp.start()
    up, down = lax.rem(s + 1, seqs), lax.rem(s + seqs - 1, seqs)
    chead = pltpu.make_async_remote_copy(
        cot.at[pl.ds(0, PAD)], cext.at[pl.ds(own, PAD)], hs.at[0], hr.at[0],
        device_id={"seq": down}, device_id_type=MESH)
    tail = pltpu.make_async_remote_copy(
        ext.at[:, pl.ds(own, PAD)], ext.at[:, pl.ds(0, PAD)], hs.at[1], hr.at[1],
        device_id={"seq": up}, device_id_type=MESH)
    head = pltpu.make_async_remote_copy(
        ext.at[:, pl.ds(PAD, PAD)], ext.at[:, pl.ds(PAD + own, PAD)], hs.at[2], hr.at[2],
        device_id={"seq": down}, device_id_type=MESH)
    first, last = s == 0, s == seqs - 1
    zlo = pltpu.make_async_copy(zero, ext.at[:, pl.ds(0, PAD)], lsem.at[2])
    zhi = pltpu.make_async_copy(zero, ext.at[:, pl.ds(PAD + own, PAD)], lsem.at[3])
    zc = pltpu.make_async_copy(zero.at[0], cext.at[pl.ds(own, PAD)], lsem.at[4])

    @pl.when(jnp.logical_not(first))
    def _():
        chead.start()

    @pl.when(first)
    def _():
        zlo.start()

    @pl.when(last)
    def _():
        zhi.start()
        zc.start()

    for cp in copies:
        cp.wait_recv()
    local[0].wait()

    @pl.when(jnp.logical_not(last))
    def _():
        tail.start()

    @pl.when(jnp.logical_not(first))
    def _():
        head.start()

    @pl.when(jnp.logical_not(first))
    def _():
        chead.wait_send()
        head.wait_send()
        tail.wait_recv()

    @pl.when(jnp.logical_not(last))
    def _():
        tail.wait_send()
        chead.wait_recv()
        head.wait_recv()

    @pl.when(first)
    def _():
        zlo.wait()

    @pl.when(last)
    def _():
        zhi.wait()
        zc.wait()

    local[1].wait()
    for cp in copies:
        cp.wait_send()


def return_kernel(chans, x, out, ssem, rsem, lsem):
    c = lax.axis_index("chan")
    rows = out.shape[1]
    width = x.shape[2]
    greet(chans, 0)

    def block(dst):
        return x.at[:, pl.ds(pl.multiple_of(dst * rows, 16), rows), :]

    def place(src):
        return out.at[:, :, pl.ds(pl.multiple_of(src * width, width), width)]

    copies = []
    for k in range(1, chans):
        d = lax.rem(c + k, chans)
        cp = pltpu.make_async_remote_copy(
            block(d), place(c), ssem.at[k], rsem.at[k], device_id={"chan": d}, device_id_type=MESH)
        cp.start()
        copies.append(cp)
    local = pltpu.make_async_copy(block(c), place(c), lsem)
    local.start()
    local.wait()
    for cp in copies:
        cp.wait()


def mix_kernel(own, ext, cext, taps, filt, filt_rev, seg_col, seg_row, hy, fg,
               xs, fm, mf, mb, lf, lt, gat, gl, sh, gs):
    blocks = own // MEDIUM
    sizes = [MEDIUM] * blocks + [TAIL]
    grow = own + PAD

    @pl.when(pl.program_id(0) == 0)
    def _():
        for j in range(1, SHORT):
            n = fm.shape[1] - 8
            same = seg_col[pl.ds(8, n), :] == seg_col[pl.ds(8 - j, n), :]
            fm[j - 1, pl.ds(8, n), :] = jnp.where(same, 1.0, 0.0)
        for b, rows in enumerate(sizes):
            r = lax.broadcasted_iota(jnp.int32, (rows, 2 * MEDIUM), 0)
            k = lax.broadcasted_iota(jnp.int32, (rows, 2 * MEDIUM), 1)
            here = jnp.tile(seg_col[pl.ds(PAD + MEDIUM * b, rows), :], (1, 2))
            past = jnp.broadcast_to(seg_row[0:1, pl.ds(MEDIUM * b, 2 * MEDIUM)], (rows, 2 * MEDIUM))
            lag = r + MEDIUM - k
            ok = (lag >= 0) & (lag < MEDIUM) & (here == past)
            mf[b, pl.ds(0, rows), :] = jnp.where(ok, 1.0, 0.0).astype(jnp.bfloat16)
            ahead = jnp.broadcast_to(seg_row[0:1, pl.ds(MEDIUM * (b + 1), 2 * MEDIUM)], (rows, 2 * MEDIUM))
            lag = k - r
            ok = (lag >= 0) & (lag < MEDIUM) & (here == ahead)
            mb[b, pl.ds(0, rows), :] = jnp.where(ok, 1.0, 0.0).astype(jnp.bfloat16)
        gat[...] = jnp.zeros_like(gat)
        gl[...] = jnp.zeros_like(gl)

    xs[...] = ext[...].astype(jnp.float32)
    coef = [[taps[m, j : j + 1, :] for j in range(SHORT)] for m in range(3)]

    def short(m, start, rows):
        total = coef[m][0] * xs[m, pl.ds(start, rows), :]
        for j in range(1, SHORT):
            total = total + coef[m][j] * (
                fm[j - 1, pl.ds(start, rows), :] * xs[m, pl.ds(start - j, rows), :])
        return total

    step = 80
    for at in range(0, grow, step):
        q = short(0, PAD + at, step)
        if at < own + TAIL:
            n = min(step, own + TAIL - at)
            sh[0, pl.ds(at, n), :] = q[:n]
        gl[pl.ds(at, step), :] = (cext[pl.ds(at, step), :].astype(jnp.float32) * q).astype(jnp.bfloat16)
    for at in range(0, grow, step):
        k = short(1, PAD - MEDIUM + at, step)
        v = short(2, PAD - MEDIUM + at, step)
        gat[pl.ds(at, step), :] = (k * v).astype(jnp.bfloat16)
        lo = max(0, MEDIUM - at)
        if lo < step:
            sh[1, pl.ds(at + lo - MEDIUM, step - lo), :] = k[lo:]
            sh[2, pl.ds(at + lo - MEDIUM, step - lo), :] = v[lo:]

    lane_group = lax.broadcasted_iota(jnp.int32, (MEDIUM, LANES), 1) // (LANES // 8)

    def band(filters, masks):
        for g in range(8):
            row = jnp.broadcast_to(filters[g : g + 1, :], (MEDIUM, MEDIUM))
            circ = pltpu.roll(row, 0, 1, stride=1, stride_axis=0).astype(jnp.bfloat16)
            two = jnp.concatenate([circ, circ], axis=1)
            for b in range(blocks):
                lf[b, pl.ds(g * MEDIUM, MEDIUM), :] = two * masks[b]
            lt[pl.ds(g * TAIL, TAIL), :] = two[:TAIL] * masks[blocks, pl.ds(0, TAIL), :]

    def product(b, source):
        rhs = source[pl.ds(MEDIUM * b, 2 * MEDIUM), :]
        rows = sizes[b]
        lhs = lf[b] if b < blocks else lt[...]
        res = jnp.dot(lhs, rhs, preferred_element_type=jnp.float32)
        total = res[:rows]
        for g in range(1, 8):
            total = jnp.where(lane_group[:rows] == g, res[g * rows : (g + 1) * rows], total)
        return total

    band(filt_rev, mf)
    for b, rows in enumerate(sizes):
        long = product(b, gat)
        at = pl.ds(MEDIUM * b, rows)
        if b < blocks:
            hy[at, :] = (sh[0, at, :] * long).astype(jnp.bfloat16)
        gs[0, at, :] = cext[at, :].astype(jnp.float32) * long
    band(filt, mb)
    for b, rows in enumerate(sizes):
        back = product(b, gl)
        at = pl.ds(MEDIUM * b, rows)
        gs[1, at, :] = back * sh[2, at, :]
        gs[2, at, :] = back * sh[1, at, :]

    for m in range(3):
        for at in range(0, own, 64):
            total = coef[m][0] * gs[m, pl.ds(at, 64), :]
            for j in range(1, SHORT):
                total = total + coef[m][j] * (
                    fm[j - 1, pl.ds(PAD + at + j, 64), :] * gs[m, pl.ds(at + j, 64), :])
            fg[m, pl.ds(at, 64), :] = total.astype(jnp.bfloat16)


def solution(mesh):
    chans, seqs = mesh.shape["chan"], mesh.shape["seq"]

    def body(features, cotangent, short_filter, medium_filter, doc_start):
        own, width = cotangent.shape
        rows, _, full = features.shape
        groups = medium_filter.shape[0]
        grow = own + PAD
        total = own + 2 * PAD
        bf, f32 = jnp.bfloat16, jnp.float32
        x = jnp.transpose(features, (1, 0, 2))
        zero = jnp.zeros((3, PAD, width), bf)
        dma = pltpu.SemaphoreType.DMA
        ext, cext = pl.pallas_call(
            functools.partial(gather_kernel, chans, seqs),
            out_shape=(jax.ShapeDtypeStruct((3, total, width), bf), jax.ShapeDtypeStruct((grow, width), bf)),
            in_specs=[ANY] * 3,
            out_specs=(ANY, ANY),
            scratch_shapes=[dma((chans,)), dma((chans,)), dma((5,)), dma((3,)), dma((3,))],
            compiler_params=pltpu.CompilerParams(collective_id=0, has_side_effects=True),
            name="gather_parts",
        )(x, cotangent, zero)
        span = total + MEDIUM
        pos = lax.axis_index("seq") * own - PAD + jnp.arange(span, dtype=jnp.int32)
        bounds = jnp.arange(doc_start.shape[0], dtype=jnp.int32) * own + doc_start
        seg = jnp.sum((bounds[None, :] <= pos[:, None]).astype(jnp.int32), axis=1)
        seg_col = jnp.broadcast_to(seg[:total, None], (total, LANES))
        reach = own + 3 * MEDIUM
        seg_row = jnp.broadcast_to(seg[PAD - MEDIUM : PAD - MEDIUM + reach][None], (8, reach))
        taps = jnp.repeat(jnp.transpose(short_filter, (0, 2, 1)), width // groups, axis=2)
        taps = jnp.pad(taps, ((0, 0), (0, 1), (0, 0)))
        filt = medium_filter.astype(bf).astype(f32)
        filt_rev = jnp.roll(filt[:, ::-1], 1, axis=1)
        blocks = own // MEDIUM
        whole = lambda shape: pl.BlockSpec(shape, lambda i: (0,) * len(shape))
        hy, fg = pl.pallas_call(
            functools.partial(mix_kernel, own),
            grid=(width // LANES,),
            out_shape=(jax.ShapeDtypeStruct((own, width), bf), jax.ShapeDtypeStruct((3, own, width), bf)),
            in_specs=[
                pl.BlockSpec((3, total, LANES), lambda i: (0, 0, i)),
                pl.BlockSpec((grow, LANES), lambda i: (0, i)),
                pl.BlockSpec((3, 8, LANES), lambda i: (0, 0, i)),
                pl.BlockSpec((8, MEDIUM), lambda i: (i, 0)),
                pl.BlockSpec((8, MEDIUM), lambda i: (i, 0)),
                whole((total, LANES)),
                whole((8, reach)),
            ],
            out_specs=(
                pl.BlockSpec((own, LANES), lambda i: (0, i)),
                pl.BlockSpec((3, own, LANES), lambda i: (0, 0, i)),
            ),
            scratch_shapes=[
                pltpu.VMEM((3, total, LANES), f32),
                pltpu.VMEM((SHORT - 1, total, LANES), f32),
                pltpu.VMEM((blocks + 1, MEDIUM, 2 * MEDIUM), bf),
                pltpu.VMEM((blocks + 1, MEDIUM, 2 * MEDIUM), bf),
                pltpu.VMEM((blocks, 8 * MEDIUM, 2 * MEDIUM), bf),
                pltpu.VMEM((8 * TAIL, 2 * MEDIUM), bf),
                pltpu.VMEM((own + 2 * MEDIUM, LANES), bf),
                pltpu.VMEM((own + 2 * MEDIUM, LANES), bf),
                pltpu.VMEM((3, own + TAIL, LANES), f32),
                pltpu.VMEM((3, own + TAIL, LANES), f32),
            ],
            compiler_params=pltpu.CompilerParams(
                dimension_semantics=("arbitrary",), vmem_limit_bytes=40 << 20),
            name="mix_tile",
        )(ext, cext, taps, filt, filt_rev, seg_col, seg_row)
        back = pl.pallas_call(
            functools.partial(return_kernel, chans),
            out_shape=jax.ShapeDtypeStruct((3, rows, full), bf),
            in_specs=[ANY],
            out_specs=ANY,
            scratch_shapes=[dma((chans,)), dma((chans,)), dma],
            compiler_params=pltpu.CompilerParams(collective_id=1, has_side_effects=True),
            name="return_parts",
        )(fg)
        return hy, jnp.transpose(back, (1, 0, 2))

    in_specs = (
        P(("seq", "chan"), None, None),
        P("seq", "chan"),
        P(None, "chan", None),
        P("chan", None),
        P(),
    )
    out_specs = (P("seq", "chan"), P(("seq", "chan"), None, None))
    return jax.shard_map(body, mesh=mesh, in_specs=in_specs, out_specs=out_specs, check_vma=False)
```

time: 722 us -> 209 us (0.29)
  the two profiles are of different devices: /device:TPU:0 before, /device:TPU:29 now
where the time goes in v1:
time: 209 us
  Pallas kernels  193 us (92%)
  local copies, waits for them, and re-layouts  13.6 us (7%)
    pallas_call x1, Pallas kernels, body(): pl.pallas_call(functools.partial(gather_kernel, chans, seqs), out_shape=(...  130 us
    pallas_call x1, Pallas kernels, body(): pl.pallas_call(functools.partial(return_kernel, chans), out_shape=jax.Sha...  36.8 us
    pallas_call x1, Pallas kernels, body(): pl.pallas_call(functools.partial(mix_kernel, own), grid=(width // LANES,)...  26.2 us
    unnamed x7, local copies, waits for them, and re-layouts  9.84 us

profile of v1, /device:TPU:29, one launch (start us, length us, event | category | flops | bytes accessed | tf_op | source)
XLA Modules:
  0.0 209.0 jit_solution(13331236561946279118)
XLA Ops:
  0.6 0.7 multiply_add_fusion
  1.3 0.1 convert_reduce_fusion
  1.4 0.1 slice.22
  1.5 0.8 convert_convert_fusion.filt
  2.3 0.1 slice.24
  2.4 0.1 slice.20
  2.5 0.1 pad_maximum_fusion.filt_rev
  2.6 0.1 broadcast_in_dim.10.seg_col
  2.7 1.1 broadcast_in_dim.9
  3.8 0.8 reshape.14
  4.6 1.4 broadcast_in_dim.8.zero
  6.1 130.1 %gather_parts.1 = (bf16[3,544,2048]{2,1,0:T(8,128)(2,1)}, bf16[400,2048]{1,0:T(8,128)(2,1)}) custom-call(bf16[3,64,8192]{2,1,0:T(8,128)(2,1)} %bitcast.9, bf16[256,2048]{1,0:T(8,128)(2,1)} %cot.1, bf16[3,144,2048]{2,1,0:T(8,128)(2,1)} %broadcast_in_dim.8.zero), custom_call_target="tpu_custom_call" | custom-call | tf_op jit(solution)/shard_map/gather_parts/pallas_call | solution.py:260
  136.2 0.0 copy-start
  136.2 2.9 %copy-done = bf16[3,544,2048]{2,1,0:T(8,128)(2,1)S(1)} copy-done((bf16[3,544,2048]{2,1,0:T(8,128)(2,1)S(1)}, bf16[3,544,2048]{2,1,0:T(8,128)(2,1)}, u32[]{:S(2)}) %copy-start) | copy-done | bytes 6684696
  139.1 0.0 copy-start.2
  139.1 1.4 copy-done.2
  140.5 26.2 %mix_tile.1 = (bf16[256,2048]{1,0:T(8,128)(2,1)}, bf16[3,256,2048]{2,1,0:T(8,128)(2,1)S(1)}) custom-call(bf16[3,544,2048]{2,1,0:T(8,128)(2,1)S(1)} %copy-done, bf16[400,2048]{1,0:T(8,128)(2,1)S(1)} %copy-done.2, f32[3,8,2048]{2,1,0:T(8,128)S(1)} %pad.4.taps, f32[128,128]{1,0:T(8,128)S(1)} %convert_convert_fusion.filt, ...), custom_call_target="tpu_custom_call" | custom-call | tf_op jit(solution)/shard_map/mix_tile/pallas_call | solution.py:282
  166.7 0.0 copy-start.1
  166.7 1.7 copy-done.1
  168.4 36.8 %return_parts.1 = bf16[3,64,8192]{2,1,0:T(8,128)(2,1)} custom-call(bf16[3,256,2048]{2,1,0:T(8,128)(2,1)} %copy-done.1), custom_call_target="tpu_custom_call" | custom-call | tf_op jit(solution)/shard_map/return_parts/pallas_call | solution.py:315
  205.2 3.9 %copy.8 = bf16[64,3,8192]{2,0,1:T(8,128)(2,1)} copy(bf16[64,3,8192]{2,0,1:T(8,128)(2,1)} %bitcast.8) | data formatting | bytes 6291456
  (3 shorter events, 0.0 us)
Async XLA Ops:
  136.2 2.9 %copy-start = (bf16[3,544,2048]{2,1,0:T(8,128)(2,1)S(1)}, bf16[3,544,2048]{2,1,0:T(8,128)(2,1)}, u32[]{:S(2)}) copy-start(bf16[3,544,2048]{2,1,0:T(8,128)(2,1)} %get-tuple-element.6.ext) | copy-start | bytes 20054020
  139.1 1.4 copy-start.2
  166.7 1.7 copy-start.1

commit v2 on v1

v2 whole, which is shorter than its diff:
```python
import functools

import jax
import jax.numpy as jnp
from jax import lax
from jax.experimental import pallas as pl
from jax.experimental.pallas import tpu as pltpu
from jax.sharding import PartitionSpec as P

SHORT = 7
MEDIUM = 128
EDGE = 8
TAIL = 16
GROW = MEDIUM + TAIL
LANES = 128
WIDE = 1024
FAR = 1 << 20
MESH = pl.DeviceIdType.MESH
ANY = pl.BlockSpec(memory_space=pl.ANY)


def spot():
    return lax.axis_index("chan"), lax.axis_index("seq")


def greet(chans, seqs, ring, line):
    c, s = spot()
    bar = pltpu.get_barrier_semaphore()
    for k in range(1, chans):
        pl.semaphore_signal(bar, inc=1, device_id={"chan": lax.rem(c + k, chans)}, device_id_type=MESH)
    count = chans - 1
    if ring:
        for k in (1, seqs - 1):
            pl.semaphore_signal(bar, inc=1, device_id={"seq": lax.rem(s + k, seqs)}, device_id_type=MESH)
        count += 2
    if line:
        for dev in line_ends(chans, seqs):
            pl.semaphore_signal(bar, inc=1, device_id=dev, device_id_type=MESH)
        count += 2
    pl.semaphore_wait(bar, count)


def line_ends(chans, seqs):
    c, s = spot()
    after = {"seq": lax.rem(s + (c + 1) // chans, seqs), "chan": lax.rem(c + 1, chans)}
    ahead = {"seq": lax.rem(s + seqs - 1 + (c + chans - 1) // chans, seqs), "chan": lax.rem(c + chans - 1, chans)}
    return after, ahead


def remote(src, dst, ssem, rsem, dev):
    return pltpu.make_async_remote_copy(src, dst, ssem, rsem, device_id=dev, device_id_type=MESH)


def first_kernel(chans, seqs, x, cot, ctaps, q, xprev, xnext, taps, cnext, ssem, rsem, tsem, usem, hs, hr, lsem):
    c, s = spot()
    rows = x.shape[1]
    width = q.shape[1]
    greet(chans, seqs, True, True)
    after, ahead = line_ends(chans, seqs)
    copies = [
        remote(x.at[pl.ds(1, 2), pl.ds(rows - EDGE, EDGE)], xprev, hs.at[0], hr.at[0], after),
        remote(x.at[pl.ds(1, 2), pl.ds(0, EDGE)], xnext, hs.at[1], hr.at[1], ahead),
        remote(cot.at[pl.ds(0, GROW)], cnext, hs.at[2], hr.at[2], {"seq": lax.rem(s + seqs - 1, seqs)}),
    ]
    for k in range(1, chans):
        d = lax.rem(c + k, chans)
        copies.append(remote(ctaps, taps.at[c], tsem.at[k], usem.at[k], {"chan": d}))
    place = q.at[pl.ds(pl.multiple_of(c * rows, 16), rows)]
    for k in range(1, chans):
        d = lax.rem(c + k, chans)
        part = x.at[0, :, pl.ds(pl.multiple_of(d * width, width), width)]
        copies.append(remote(part, place, ssem.at[k], rsem.at[k], {"chan": d}))
    mine = x.at[0, :, pl.ds(pl.multiple_of(c * width, width), width)]
    copies.append(pltpu.make_async_copy(mine, place, lsem.at[0]))
    copies.append(pltpu.make_async_copy(ctaps, taps.at[c], lsem.at[1]))
    for cp in copies:
        cp.start()
    for cp in copies:
        cp.wait()


def second_kernel(chans, seqs, q, gated, gown, gprev, gnext, qprev, qnext, ssem, rsem, hs, hr, lsem):
    c, s = spot()
    rows = gated.shape[0]
    own, width = q.shape
    greet(chans, seqs, True, False)
    up, down = {"seq": lax.rem(s + 1, seqs)}, {"seq": lax.rem(s + seqs - 1, seqs)}
    place = gown.at[pl.ds(pl.multiple_of(c * rows, 16), rows)]
    main = []
    for k in range(1, chans):
        d = lax.rem(c + k, chans)
        part = gated.at[:, pl.ds(pl.multiple_of(d * width, width), width)]
        main.append(remote(part, place, ssem.at[k], rsem.at[k], {"chan": d}))
    mine = gated.at[:, pl.ds(pl.multiple_of(c * width, width), width)]
    local = pltpu.make_async_copy(mine, place, lsem)
    side = [
        remote(q.at[pl.ds(own - TAIL, TAIL)], qprev, hs.at[0], hr.at[0], up),
        remote(q.at[pl.ds(0, GROW)], qnext, hs.at[1], hr.at[1], down),
    ]
    for cp in main + [local] + side:
        cp.start()
    for cp in main:
        cp.wait_recv()
    local.wait()
    late = [
        remote(gown.at[pl.ds(own - MEDIUM, MEDIUM)], gprev, hs.at[2], hr.at[2], up),
        remote(gown.at[pl.ds(0, TAIL)], gnext, hs.at[3], hr.at[3], down),
    ]
    for cp in late:
        cp.start()
    for cp in main:
        cp.wait_send()
    for cp in side + late:
        cp.wait()


def third_kernel(chans, seqs, g, out, ssem, rsem, lsem):
    c, _ = spot()
    rows = out.shape[1]
    width = g.shape[2]
    greet(chans, seqs, False, False)
    place = out.at[:, :, pl.ds(pl.multiple_of(c * width, width), width)]

    def part(d):
        return g.at[:, pl.ds(pl.multiple_of(d * (rows - EDGE), 8), rows), :]

    copies = []
    for k in range(1, chans):
        d = lax.rem(c + k, chans)
        copies.append(remote(part(d), place, ssem.at[k], rsem.at[k], {"chan": d}))
    copies.append(pltpu.make_async_copy(part(c), place, lsem))
    for cp in copies:
        cp.start()
    for cp in copies:
        cp.wait()


def open_taps(fm, seg_col, lo, n):
    for j in range(1, SHORT):
        same = seg_col[pl.ds(lo, n), :] == seg_col[pl.ds(lo - j, n), :]
        fm[j - 1, pl.ds(0, n), :] = jnp.where(same, 1.0, 0.0)


def gate_kernel(x, xprev, xnext, taps, seg_col, gated, kv, fm, xs):
    rows = x.shape[1]
    more = rows + EDGE

    @pl.when(pl.program_id(0) == 0)
    def _():
        open_taps(fm, seg_col, EDGE, more)

    f32 = jnp.float32
    for m in range(2):
        xs[m, pl.ds(0, EDGE), :] = xprev[m].astype(f32)
        xs[m, pl.ds(EDGE, rows), :] = x[m + 1].astype(f32)
        xs[m, pl.ds(EDGE + rows, EDGE), :] = xnext[m].astype(f32)
    for t in range(x.shape[2] // LANES):
        at = pl.ds(t * LANES, LANES)
        outs = []
        for m in range(2):
            total = taps[m + 1, 0:1, at] * xs[m, pl.ds(EDGE, more), at]
            for j in range(1, SHORT):
                total = total + taps[m + 1, j : j + 1, at] * (
                    fm[j - 1] * xs[m, pl.ds(EDGE - j, more), at])
            kv[m, :, at] = total
            outs.append(total[:rows])
        gated[:, at] = (outs[0] * outs[1]).astype(jnp.bfloat16)


def last_kernel(g, kv, taps, seg_col, out, fm, gs):
    rows = out.shape[1]
    more = rows + EDGE

    @pl.when(pl.program_id(0) == 0)
    def _():
        open_taps(fm, seg_col, EDGE, more)

    f32 = jnp.float32
    gs[0] = g[0].astype(f32)
    back = g[1].astype(f32)
    gs[1] = back * kv[1]
    gs[2] = back * kv[0]
    for t in range(out.shape[2] // LANES):
        at = pl.ds(t * LANES, LANES)
        for m in range(3):
            total = taps[m, 0:1, at] * gs[m, pl.ds(0, rows), at]
            for j in range(1, SHORT):
                total = total + taps[m, j : j + 1, at] * (
                    fm[j - 1, pl.ds(j, rows), :] * gs[m, pl.ds(j, rows), at])
            out[m, :, at] = total.astype(jnp.bfloat16)


def mix_kernel(own, q, qprev, qnext, gown, gprev, gnext, cot, cnext, taps, filt, filt_rev, seg_col, seg_row,
               hy, grads, xs, fm, mf, mb, lf, lt, gat, gl, sh, cs):
    blocks = own // MEDIUM
    sizes = [MEDIUM] * blocks + [TAIL]
    grow = own + GROW
    f32 = jnp.float32

    @pl.when(pl.program_id(0) == 0)
    def _():
        open_taps(fm, seg_col, TAIL, grow)
        for b, rows in enumerate(sizes):
            r = lax.broadcasted_iota(jnp.int32, (rows, 2 * MEDIUM), 0)
            k = lax.broadcasted_iota(jnp.int32, (rows, 2 * MEDIUM), 1)
            here = jnp.tile(seg_col[pl.ds(TAIL + MEDIUM * b, rows), :], (1, 2))
            past = jnp.broadcast_to(seg_row[0:1, pl.ds(MEDIUM * b, 2 * MEDIUM)], (rows, 2 * MEDIUM))
            lag = r + MEDIUM - k
            ok = (lag >= 0) & (lag < MEDIUM) & (here == past)
            mf[b, pl.ds(0, rows), :] = jnp.where(ok, 1.0, 0.0).astype(jnp.bfloat16)
            ahead = jnp.broadcast_to(seg_row[0:1, pl.ds(MEDIUM * (b + 1), 2 * MEDIUM)], (rows, 2 * MEDIUM))
            lag = k - r
            ok = (lag >= 0) & (lag < MEDIUM) & (here == ahead)
            mb[b, pl.ds(0, rows), :] = jnp.where(ok, 1.0, 0.0).astype(jnp.bfloat16)
        gat[...] = jnp.zeros_like(gat)
        gl[...] = jnp.zeros_like(gl)

    xs[pl.ds(0, TAIL), :] = qprev[...].astype(f32)
    xs[pl.ds(TAIL, own), :] = q[...].astype(f32)
    xs[pl.ds(TAIL + own, GROW), :] = qnext[...].astype(f32)
    cs[pl.ds(0, own), :] = cot[...].astype(f32)
    cs[pl.ds(own, GROW), :] = cnext[...].astype(f32)
    gat[pl.ds(0, MEDIUM), :] = gprev[...]
    gat[pl.ds(MEDIUM, own), :] = gown[...]
    gat[pl.ds(MEDIUM + own, TAIL), :] = gnext[...]
    coef = [taps[0, j : j + 1, :] for j in range(SHORT)]
    step = 80
    for at in range(0, grow, step):
        total = coef[0] * xs[pl.ds(TAIL + at, step), :]
        for j in range(1, SHORT):
            total = total + coef[j] * (fm[j - 1, pl.ds(at, step), :] * xs[pl.ds(TAIL + at - j, step), :])
        if at < own:
            n = min(step, own - at)
            sh[pl.ds(at, n), :] = total[:n]
        gl[pl.ds(at, step), :] = (cs[pl.ds(at, step), :] * total).astype(jnp.bfloat16)

    lane_group = lax.broadcasted_iota(jnp.int32, (MEDIUM, LANES), 1) // (LANES // 8)

    def band(filters, masks):
        for g in range(8):
            row = jnp.broadcast_to(filters[g : g + 1, :], (MEDIUM, MEDIUM))
            circ = pltpu.roll(row, 0, 1, stride=1, stride_axis=0).astype(jnp.bfloat16)
            two = jnp.concatenate([circ, circ], axis=1)
            for b in range(blocks):
                lf[b, pl.ds(g * MEDIUM, MEDIUM), :] = two * masks[b]
            lt[pl.ds(g * TAIL, TAIL), :] = two[:TAIL] * masks[blocks, pl.ds(0, TAIL), :]

    def product(b, source):
        rhs = source[pl.ds(MEDIUM * b, 2 * MEDIUM), :]
        rows = sizes[b]
        lhs = lf[b] if b < blocks else lt[...]
        res = jnp.dot(lhs, rhs, preferred_element_type=f32)
        total = res[:rows]
        for g in range(1, 8):
            total = jnp.where(lane_group[:rows] == g, res[g * rows : (g + 1) * rows], total)
        return total

    band(filt_rev, mf)
    for b, rows in enumerate(sizes):
        long = product(b, gat)
        at = pl.ds(MEDIUM * b, rows)
        if b < blocks:
            hy[at, :] = (sh[at, :] * long).astype(jnp.bfloat16)
        grads[0, at, :] = (cs[at, :] * long).astype(jnp.bfloat16)
    band(filt, mb)
    for b, rows in enumerate(sizes):
        grads[1, pl.ds(MEDIUM * b, rows), :] = product(b, gl).astype(jnp.bfloat16)


def solution(mesh):
    chans, seqs = mesh.shape["chan"], mesh.shape["seq"]

    def body(features, cotangent, short_filter, medium_filter, doc_start):
        own, width = cotangent.shape
        rows, _, full = features.shape
        groups = medium_filter.shape[0]
        span = full // (groups * chans)
        grow = own + GROW
        more = rows + EDGE
        bf, f32 = jnp.bfloat16, jnp.float32
        shape = jax.ShapeDtypeStruct
        dma = pltpu.SemaphoreType.DMA
        x = jnp.transpose(features, (1, 0, 2))
        ctaps = jnp.pad(jnp.transpose(short_filter, (0, 2, 1)), ((0, 0), (0, 1), (0, 0)))
        q, xprev, xnext, taps, cnext = pl.pallas_call(
            functools.partial(first_kernel, chans, seqs),
            out_shape=(
                shape((own, width), bf), shape((2, EDGE, full), bf), shape((2, EDGE, full), bf),
                shape((chans, 3, 8, groups), f32), shape((GROW, width), bf)),
            in_specs=[ANY] * 3,
            out_specs=(ANY,) * 5,
            scratch_shapes=[dma((chans,))] * 4 + [dma((3,)), dma((3,)), dma((2,))],
            compiler_params=pltpu.CompilerParams(collective_id=0, has_side_effects=True),
            name="first_parts",
        )(x, cotangent, ctaps)
        taps = jnp.repeat(jnp.transpose(taps, (1, 2, 0, 3)).reshape(3, 8, groups * chans), span, axis=2)
        mytaps = jnp.repeat(ctaps[:1], span, axis=2)

        tokens = own * seqs
        bounds = jnp.arange(doc_start.shape[0], dtype=jnp.int32) * own + doc_start

        def ids(base, n):
            pos = base + jnp.arange(n, dtype=jnp.int32)
            seg = jnp.sum((bounds[None, :] <= pos[:, None]).astype(jnp.int32), axis=1)
            return jnp.where(pos < 0, -1, jnp.where(pos >= tokens, FAR, seg))

        start = lax.axis_index("seq") * own
        seg = ids(start - MEDIUM, own + 3 * MEDIUM)
        cols = TAIL + grow
        seg_col = jnp.broadcast_to(seg[MEDIUM - TAIL : MEDIUM - TAIL + cols, None], (cols, LANES))
        seg_row = jnp.broadcast_to(seg[None], (8, seg.shape[0]))
        rseg = ids(start + lax.axis_index("chan") * rows - EDGE, rows + 2 * EDGE)
        rseg_col = jnp.broadcast_to(rseg[:, None], (rseg.shape[0], LANES))
        filt = medium_filter.astype(bf).astype(f32)
        filt_rev = jnp.roll(filt[:, ::-1], 1, axis=1)

        whole = lambda dims: pl.BlockSpec(dims, lambda i: (0,) * len(dims))
        flat = lambda n, w: pl.BlockSpec((n, w), lambda i: (0, i))
        cube = lambda m, n, w: pl.BlockSpec((m, n, w), lambda i: (0, 0, i))
        gated, kv = pl.pallas_call(
            gate_kernel,
            grid=(full // WIDE,),
            out_shape=(shape((rows, full), bf), shape((2, more, full), f32)),
            in_specs=[cube(3, rows, WIDE), cube(2, EDGE, WIDE), cube(2, EDGE, WIDE), cube(3, 8, WIDE),
                      whole(rseg_col.shape)],
            out_specs=(flat(rows, WIDE), cube(2, more, WIDE)),
            scratch_shapes=[pltpu.VMEM((SHORT - 1, more, LANES), f32),
                            pltpu.VMEM((2, rows + 2 * EDGE, WIDE), f32)],
            compiler_params=pltpu.CompilerParams(vmem_limit_bytes=40 << 20),
            name="gate_rows",
        )(x, xprev, xnext, taps, rseg_col)

        gown, gprev, gnext, qprev, qnext = pl.pallas_call(
            functools.partial(second_kernel, chans, seqs),
            out_shape=tuple(shape((n, width), bf) for n in (own, MEDIUM, TAIL, TAIL, GROW)),
            in_specs=[ANY] * 2,
            out_specs=(ANY,) * 5,
            scratch_shapes=[dma((chans,))] * 2 + [dma((4,)), dma((4,)), dma],
            compiler_params=pltpu.CompilerParams(collective_id=1, has_side_effects=True),
            name="second_parts",
        )(q, gated)

        blocks = own // MEDIUM
        hy, grads = pl.pallas_call(
            functools.partial(mix_kernel, own),
            grid=(width // LANES,),
            out_shape=(shape((own, width), bf), shape((2, own + TAIL, width), bf)),
            in_specs=[
                flat(own, LANES), flat(TAIL, LANES), flat(GROW, LANES),
                flat(own, LANES), flat(MEDIUM, LANES), flat(TAIL, LANES),
                flat(own, LANES), flat(GROW, LANES),
                cube(1, 8, LANES),
                pl.BlockSpec((8, MEDIUM), lambda i: (i, 0)),
                pl.BlockSpec((8, MEDIUM), lambda i: (i, 0)),
                whole(seg_col.shape), whole(seg_row.shape),
            ],
            out_specs=(flat(own, LANES), cube(2, own + TAIL, LANES)),
            scratch_shapes=[
                pltpu.VMEM((cols, LANES), f32),
                pltpu.VMEM((SHORT - 1, grow, LANES), f32),
                pltpu.VMEM((blocks + 1, MEDIUM, 2 * MEDIUM), bf),
                pltpu.VMEM((blocks + 1, MEDIUM, 2 * MEDIUM), bf),
                pltpu.VMEM((blocks, 8 * MEDIUM, 2 * MEDIUM), bf),
                pltpu.VMEM((8 * TAIL, 2 * MEDIUM), bf),
                pltpu.VMEM((own + 2 * MEDIUM, LANES), bf),
                pltpu.VMEM((own + 2 * MEDIUM, LANES), bf),
                pltpu.VMEM((own, LANES), f32),
                pltpu.VMEM((grow, LANES), f32),
            ],
            compiler_params=pltpu.CompilerParams(vmem_limit_bytes=40 << 20),
            name="mix_tile",
        )(q, qprev, qnext, gown, gprev, gnext, cotangent, cnext, mytaps, filt, filt_rev, seg_col, seg_row)

        back = pl.pallas_call(
            functools.partial(third_kernel, chans, seqs),
            out_shape=shape((2, more, full), bf),
            in_specs=[ANY],
            out_specs=ANY,
            scratch_shapes=[dma((chans,)), dma((chans,)), dma],
            compiler_params=pltpu.CompilerParams(collective_id=2, has_side_effects=True),
            name="third_parts",
        )(grads)

        grad = pl.pallas_call(
            last_kernel,
            grid=(full // WIDE,),
            out_shape=shape((3, rows, full), bf),
            in_specs=[cube(2, more, WIDE), cube(2, more, WIDE), cube(3, 8, WIDE), whole(rseg_col.shape)],
            out_specs=cube(3, rows, WIDE),
            scratch_shapes=[pltpu.VMEM((SHORT - 1, more, LANES), f32), pltpu.VMEM((3, more, WIDE), f32)],
            compiler_params=pltpu.CompilerParams(vmem_limit_bytes=40 << 20),
            name="last_rows",
        )(back, kv, taps, rseg_col)
        return hy, jnp.transpose(grad, (1, 0, 2))

    in_specs = (
        P(("seq", "chan"), None, None),
        P("seq", "chan"),
        P(None, "chan", None),
        P("chan", None),
        P(),
    )
    out_specs = (P("seq", "chan"), P(("seq", "chan"), None, None))
    return jax.shard_map(body, mesh=mesh, in_specs=in_specs, out_specs=out_specs, check_vma=False)
```

time: 209 us -> 153 us (0.73)
  the two profiles are of different devices: /device:TPU:29 before, /device:TPU:0 now
where the time goes in v2:
time: 153 us; the launch traced here: 152 us
  Pallas kernels  114 us (75%)
  local copies, waits for them, and re-layouts  36.1 us (24%)
  other arithmetic  1.8 us (1%)
    pallas_call x1, Pallas kernels, body(): pl.pallas_call(functools.partial(second_kernel, chans, seqs), out_shape=t...  30.6 us
    pallas_call x1, Pallas kernels, body(): pl.pallas_call(functools.partial(third_kernel, chans, seqs), out_shape=sh...  29.1 us
    pallas_call x1, Pallas kernels, body(): pl.pallas_call(functools.partial(first_kernel, chans, seqs), out_shape=(s...  22.1 us
    unnamed x38, local copies, waits for them, and re-layouts  20.8 us
    pallas_call x1, Pallas kernels, body(): pl.pallas_call(functools.partial(mix_kernel, own), grid=(width // LANES,)...  16.9 us
    pallas_call x1, Pallas kernels, body(): pl.pallas_call(last_kernel, grid=(full // WIDE,), out_shape=shape((3, row...  8.67 us
    reshape x1, local copies, waits for them, and re-layouts, body(): jnp.repeat(jnp.transpose(taps, (1, 2, 0, 3)).reshape(3, 8, groups * chans...  7.27 us
    pallas_call x1, Pallas kernels, body(): pl.pallas_call(gate_kernel, grid=(full // WIDE,), out_shape=(shape((rows,...  6.28 us

profile of v2, /device:TPU:0, one launch (start us, length us, event | category | flops | bytes accessed | tf_op | source)
XLA Modules:
  0.0 152.3 jit_solution(4451320305772870701)
XLA Ops:
  2.3 1.3 pad.4.ctaps
  5.1 0.9 broadcast_in_dim.49.taps
  6.0 22.1 %first_parts.1 = (bf16[256,2048]{1,0:T(8,128)(2,1)}, bf16[2,8,8192]{2,1,0:T(8,128)(2,1)}, bf16[2,8,8192]{2,1,0:T(8,128)(2,1)}, f32[4,3,8,128]{3,2,1,0:T(8,128)}, bf16[144,2048]{1,0:T(8,128)(2,1)}) custom-call(bf16[3,64,8192]{2,1,0:T(8,128)(2,1)} %bitcast.13, bf16[256,2048]{1,0:T(8,128)(2,1)} %cot.3, f32[3,8,128]{2,1,0:T(8,128)} %pad.4.ctaps), custom_call_target="tpu_custom_call" | custom-call | tf_op jit(solution)/shard_map/first_parts/pallas_call | solution.py:285
  28.9 3.7 %broadcast_in_dim.44 = f32[3,8,512,16]{3,2,1,0:T(8,128)} broadcast(f32[3,8,512]{2,1,0:T(8,128)S(1)} %copy_bitcast_fusion), dimensions={0,1,2} | broadcast | bytes 835584 | tf_op jit(solution)/shard_map/broadcast_in_dim | solution.py:296
  32.6 7.3 %reshape.44.taps = f32[3,8,8192]{2,1,0:T(8,128)} reshape(f32[3,8,512,16]{3,2,1,0:T(8,128)} %broadcast_in_dim.44) | data formatting | bytes 1572864 | tf_op jit(solution)/shard_map/reshape | solution.py:296
  39.9 1.1 copy-done.2
  41.0 0.9 copy-done.15
  42.0 0.9 copy-done.16
  42.9 6.3 %gate_rows.1 = (bf16[64,8192]{1,0:T(8,128)(2,1)S(1)}, f32[2,72,8192]{2,1,0:T(8,128)S(1)}) custom-call(bf16[3,64,8192]{2,1,0:T(8,128)(2,1)S(1)} %bitcast.14, bf16[2,8,8192]{2,1,0:T(8,128)(2,1)S(1)} %copy-done.15, bf16[2,8,8192]{2,1,0:T(8,128)(2,1)S(1)} %copy-done.16, f32[3,8,8192]{2,1,0:T(8,128)S(1)} %copy-done.2, s32[80,128]{1,0:T(8,128)S(1)} %broadcast_in_dim.47.seg_col), custom_call_target="tpu_custom_call" | custom-call | tf_op jit(solution)/shard_map/gate_rows/pallas_call | solution.py:320
  49.2 2.1 %copy-done.4 = f32[2,72,8192]{2,1,0:T(8,128)} copy-done((f32[2,72,8192]{2,1,0:T(8,128)}, f32[2,72,8192]{2,1,0:T(8,128)S(1)}, u32[]{:S(2)}) %copy-start.4) | copy-done | bytes 4718616
  51.3 1.0 copy-done.9
  52.3 30.6 %second_parts.1 = (bf16[256,2048]{1,0:T(8,128)(2,1)}, bf16[128,2048]{1,0:T(8,128)(2,1)}, bf16[16,2048]{1,0:T(8,128)(2,1)}, bf16[16,2048]{1,0:T(8,128)(2,1)}, bf16[144,2048]{1,0:T(8,128)(2,1)}) custom-call(bf16[256,2048]{1,0:T(8,128)(2,1)} %get-tuple-element.16.q, bf16[64,8192]{1,0:T(8,128)(2,1)} %copy-done.9), custom_call_target="tpu_custom_call" | custom-call | tf_op jit(solution)/shard_map/second_parts/pallas_call | solution.py:333
  82.9 1.2 copy-done.6
  84.1 1.2 copy-done.7
  85.4 1.2 copy-done.10
  86.6 1.1 copy-done.11
  87.6 1.1 copy-done.12
  88.7 1.0 copy-done.13
  92.3 16.9 %mix_tile.1 = (bf16[256,2048]{1,0:T(8,128)(2,1)}, bf16[2,272,2048]{2,1,0:T(8,128)(2,1)S(1)}) custom-call(bf16[256,2048]{1,0:T(8,128)(2,1)S(1)} %copy-done.7, bf16[16,2048]{1,0:T(8,128)(2,1)S(1)} %copy-done.18, bf16[144,2048]{1,0:T(8,128)(2,1)S(1)} %copy-done.12, bf16[256,2048]{1,0:T(8,128)(2,1)S(1)} %copy-done.10, bf16[128,2048]{1,0:T(8,128)(2,1)S(1)} %copy-done.13, ...), custom_call_target="tpu_custom_call" | custom-call | tf_op jit(solution)/shard_map/mix_tile/pallas_call | solution.py:344
  109.2 1.4 copy-done.8
  110.5 29.1 %third_parts.1.g = bf16[2,72,8192]{2,1,0:T(8,128)(2,1)} custom-call(bf16[2,272,2048]{2,1,0:T(8,128)(2,1)} %copy-done.8), custom_call_target="tpu_custom_call" | custom-call | tf_op jit(solution)/shard_map/third_parts/pallas_call | solution.py:374
  139.7 1.7 %copy-done.1 = bf16[2,72,8192]{2,1,0:T(8,128)(2,1)S(1)} copy-done((bf16[2,72,8192]{2,1,0:T(8,128)(2,1)S(1)}, bf16[2,72,8192]{2,1,0:T(8,128)(2,1)}, u32[]{:S(2)}) %copy-start.1) | copy-done | bytes 2359320
  141.3 2.3 %copy-done.5 = f32[2,72,8192]{2,1,0:T(8,128)S(1)} copy-done((f32[2,72,8192]{2,1,0:T(8,128)S(1)}, f32[2,72,8192]{2,1,0:T(8,128)}, u32[]{:S(2)}) %copy-start.5) | copy-done | bytes 4718616
  143.7 8.7 %last_rows.1 = bf16[3,64,8192]{2,1,0:T(8,128)(2,1)} custom-call(bf16[2,72,8192]{2,1,0:T(8,128)(2,1)S(1)} %copy-done.1, f32[2,72,8192]{2,1,0:T(8,128)S(1)} %copy-done.5, f32[3,8,8192]{2,1,0:T(8,128)S(1)} %copy-done.3, s32[80,128]{1,0:T(8,128)S(1)} %broadcast_in_dim.47.seg_col), custom_call_target="tpu_custom_call" | custom-call | tf_op jit(solution)/shard_map/last_rows/pallas_call | solution.py:384
  (42 shorter events, 6.4 us)
Async XLA Ops:
  32.6 7.3 %copy-start = (bf16[64,3,8192]{2,0,1:T(8,128)(2,1)S(1)}, bf16[64,3,8192]{2,0,1:T(8,128)(2,1)}, u32[]{:S(2)}) copy-start(bf16[64,3,8192]{2,0,1:T(8,128)(2,1)} %param.5) | copy-start | bytes 9437188
  39.9 1.1 copy-start.2
  41.0 0.9 copy-start.15
  42.0 0.9 copy-start.16
  49.2 2.1 %copy-start.4 = (f32[2,72,8192]{2,1,0:T(8,128)}, f32[2,72,8192]{2,1,0:T(8,128)S(1)}, u32[]{:S(2)}) copy-start(f32[2,72,8192]{2,1,0:T(8,128)S(1)} %get-tuple-element.29.kv) | copy-start | bytes 14155780
  51.3 1.0 copy-start.9
  82.9 1.2 copy-start.6
  84.1 1.2 copy-start.7
  85.4 1.2 copy-start.10
  86.6 1.1 copy-start.11
  87.6 1.1 copy-start.12
  88.7 1.0 copy-start.13
  89.8 0.8 copy-start.14
  90.6 0.8 copy-start.17
  91.4 0.8 copy-start.18
  109.2 1.4 copy-start.8
  110.5 29.1 %copy-start.3 = (f32[3,8,8192]{2,1,0:T(8,128)S(1)}, f32[3,8,8192]{2,1,0:T(8,128)}, u32[]{:S(2)}) copy-start(f32[3,8,8192]{2,1,0:T(8,128)} %reshape.44.taps) | copy-start | bytes 2359300
  139.7 1.7 %copy-start.1 = (bf16[2,72,8192]{2,1,0:T(8,128)(2,1)S(1)}, bf16[2,72,8192]{2,1,0:T(8,128)(2,1)}, u32[]{:S(2)}) copy-start(bf16[2,72,8192]{2,1,0:T(8,128)(2,1)} %third_parts.1.g) | copy-start | bytes 7077892
  141.3 2.3 %copy-start.5 = (f32[2,72,8192]{2,1,0:T(8,128)S(1)}, f32[2,72,8192]{2,1,0:T(8,128)}, u32[]{:S(2)}) copy-start(f32[2,72,8192]{2,1,0:T(8,128)} %copy-done.4) | copy-start | bytes 14155780

commit v3 on v2

--- a/solution.py
+++ b/solution.py
@@ -114,25 +114,27 @@
         cp.wait()
 
 
-def third_kernel(chans, seqs, g, out, ssem, rsem, lsem):
-    c, _ = spot()
-    rows = out.shape[1]
-    width = g.shape[2]
-    greet(chans, seqs, False, False)
-    place = out.at[:, :, pl.ds(pl.multiple_of(c * width, width), width)]
-
-    def part(d):
-        return g.at[:, pl.ds(pl.multiple_of(d * (rows - EDGE), 8), rows), :]
-
-    copies = []
-    for k in range(1, chans):
-        d = lax.rem(c + k, chans)
-        copies.append(remote(part(d), place, ssem.at[k], rsem.at[k], {"chan": d}))
-    copies.append(pltpu.make_async_copy(part(c), place, lsem))
-    for cp in copies:
-        cp.start()
-    for cp in copies:
-        cp.wait()
+def expand(t, first, lanes, span):
+    bf, f32 = jnp.bfloat16, jnp.float32
+    groups = t.shape[1]
+    row = lax.broadcasted_iota(jnp.int32, (groups, lanes), 0)
+    col = lax.broadcasted_iota(jnp.int32, (groups, lanes), 1)
+    hot = jnp.where(row == first + col // span, 1.0, 0.0).astype(bf)
+    high = t.astype(bf)
+    rest = t - high.astype(f32)
+    mid = rest.astype(bf)
+    low = (rest - mid.astype(f32)).astype(bf)
+    dot = lambda part: jnp.dot(part, hot, preferred_element_type=f32)
+    return dot(high) + (dot(mid) + dot(low))
+
+
+def spread(taps, out, span):
+    chans, _, _, groups = taps.shape
+    lanes = out.shape[2]
+    per = groups * span // lanes
+    i = pl.program_id(0)
+    full = taps[i // per].reshape(24, groups)
+    out[...] = expand(full, lax.rem(i, per) * (lanes // span), lanes, span).reshape(3, 8, lanes)
 
 
 def open_taps(fm, seg_col, lo, n):
@@ -141,7 +143,8 @@
         fm[j - 1, pl.ds(0, n), :] = jnp.where(same, 1.0, 0.0)
 
 
-def gate_kernel(x, xprev, xnext, taps, seg_col, gated, kv, fm, xs):
+def gate_kernel(span, x, xprev, xnext, ctaps, seg_col, gated, kv, fm, xs, taps):
+    spread(ctaps, taps, span)
     rows = x.shape[1]
     more = rows + EDGE
 
@@ -167,7 +170,8 @@
         gated[:, at] = (outs[0] * outs[1]).astype(jnp.bfloat16)
 
 
-def last_kernel(g, kv, taps, seg_col, out, fm, gs):
+def last_kernel(span, g, kv, ctaps, seg_col, out, fm, gs, taps):
+    spread(ctaps, taps, span)
     rows = out.shape[1]
     more = rows + EDGE
 
@@ -190,15 +194,32 @@
             out[m, :, at] = total.astype(jnp.bfloat16)
 
 
-def mix_kernel(own, q, qprev, qnext, gown, gprev, gnext, cot, cnext, taps, filt, filt_rev, seg_col, seg_row,
-               hy, grads, xs, fm, mf, mb, lf, lt, gat, gl, sh, cs):
+def mix_kernel(chans, own, span, q, qprev, qnext, gown, gprev, gnext, cot, cnext, ctaps, filt, filt_rev, seg_col,
+               seg_row, hy, out, xs, fm, mf, mb, lf, lt, gat, gl, sh, cs, sent, ssem, rsem, lsem):
+    tile = pl.program_id(0)
+    c, _ = spot()
+    more = out.shape[1]
+    rows_dev = more - EDGE
+    width = out.shape[2] // chans
+    grads = sent.at[tile]
     blocks = own // MEDIUM
     sizes = [MEDIUM] * blocks + [TAIL]
     grow = own + GROW
     f32 = jnp.float32
 
-    @pl.when(pl.program_id(0) == 0)
+    def sends(t):
+        place = out.at[:, :, pl.ds(pl.multiple_of(c * width + t * LANES, LANES), LANES)]
+        part = lambda d: sent.at[t, :, pl.ds(pl.multiple_of(d * rows_dev, 8), more), :]
+        made = []
+        for k in range(1, chans):
+            d = lax.rem(c + k, chans)
+            made.append(remote(part(d), place, ssem.at[t, k], rsem.at[t, k], {"chan": d}))
+        made.append(pltpu.make_async_copy(part(c), place, lsem.at[t]))
+        return made
+
+    @pl.when(tile == 0)
     def _():
+        greet(chans, 0, False, False)
         open_taps(fm, seg_col, TAIL, grow)
         for b, rows in enumerate(sizes):
             r = lax.broadcasted_iota(jnp.int32, (rows, 2 * MEDIUM), 0)
@@ -223,7 +244,8 @@
     gat[pl.ds(0, MEDIUM), :] = gprev[...]
     gat[pl.ds(MEDIUM, own), :] = gown[...]
     gat[pl.ds(MEDIUM + own, TAIL), :] = gnext[...]
-    coef = [taps[0, j : j + 1, :] for j in range(SHORT)]
+    taps = expand(ctaps[0], tile * (LANES // span), LANES, span)
+    coef = [taps[j : j + 1, :] for j in range(SHORT)]
     step = 80
     for at in range(0, grow, step):
         total = coef[0] * xs[pl.ds(TAIL + at, step), :]
@@ -265,6 +287,18 @@
     band(filt, mb)
     for b, rows in enumerate(sizes):
         grads[1, pl.ds(MEDIUM * b, rows), :] = product(b, gl).astype(jnp.bfloat16)
+
+    for cp in sends(tile):
+        cp.start()
+
+    @pl.when(tile == pl.num_programs(0) - 1)
+    def _():
+        def finish(t, carry):
+            for cp in sends(t):
+                cp.wait()
+            return carry
+
+        lax.fori_loop(0, pl.num_programs(0), finish, 0)
 
 
 def solution(mesh):
@@ -290,11 +324,11 @@
             in_specs=[ANY] * 3,
             out_specs=(ANY,) * 5,
             scratch_shapes=[dma((chans,))] * 4 + [dma((3,)), dma((3,)), dma((2,))],
-            compiler_params=pltpu.CompilerParams(collective_id=0, has_side_effects=True),
+            compiler_params=pltpu.CompilerParams(collective_id=0, has_side_effects=True, vmem_limit_bytes=60 << 20),
             name="first_parts",
         )(x, cotangent, ctaps)
-        taps = jnp.repeat(jnp.transpose(taps, (1, 2, 0, 3)).reshape(3, 8, groups * chans), span, axis=2)
-        mytaps = jnp.repeat(ctaps[:1], span, axis=2)
+        wide = min(WIDE, width)
+        limit = 60 << 20
 
         tokens = own * seqs
         bounds = jnp.arange(doc_start.shape[0], dtype=jnp.int32) * own + doc_start
@@ -318,15 +352,15 @@
         flat = lambda n, w: pl.BlockSpec((n, w), lambda i: (0, i))
         cube = lambda m, n, w: pl.BlockSpec((m, n, w), lambda i: (0, 0, i))
         gated, kv = pl.pallas_call(
-            gate_kernel,
-            grid=(full // WIDE,),
+            functools.partial(gate_kernel, span),
+            grid=(full // wide,),
             out_shape=(shape((rows, full), bf), shape((2, more, full), f32)),
-            in_specs=[cube(3, rows, WIDE), cube(2, EDGE, WIDE), cube(2, EDGE, WIDE), cube(3, 8, WIDE),
+            in_specs=[cube(3, rows, wide), cube(2, EDGE, wide), cube(2, EDGE, wide), whole(taps.shape),
                       whole(rseg_col.shape)],
-            out_specs=(flat(rows, WIDE), cube(2, more, WIDE)),
+            out_specs=(flat(rows, wide), cube(2, more, wide)),
             scratch_shapes=[pltpu.VMEM((SHORT - 1, more, LANES), f32),
-                            pltpu.VMEM((2, rows + 2 * EDGE, WIDE), f32)],
-            compiler_params=pltpu.CompilerParams(vmem_limit_bytes=40 << 20),
+                            pltpu.VMEM((2, rows + 2 * EDGE, wide), f32), pltpu.VMEM((3, 8, wide), f32)],
+            compiler_params=pltpu.CompilerParams(vmem_limit_bytes=limit),
             name="gate_rows",
         )(x, xprev, xnext, taps, rseg_col)
 
@@ -336,25 +370,26 @@
             in_specs=[ANY] * 2,
             out_specs=(ANY,) * 5,
             scratch_shapes=[dma((chans,))] * 2 + [dma((4,)), dma((4,)), dma],
-            compiler_params=pltpu.CompilerParams(collective_id=1, has_side_effects=True),
+            compiler_params=pltpu.CompilerParams(collective_id=1, has_side_effects=True, vmem_limit_bytes=limit),
             name="second_parts",
         )(q, gated)
 
         blocks = own // MEDIUM
-        hy, grads = pl.pallas_call(
-            functools.partial(mix_kernel, own),
+        tiles = width // LANES
+        hy, back = pl.pallas_call(
+            functools.partial(mix_kernel, chans, own, span),
             grid=(width // LANES,),
-            out_shape=(shape((own, width), bf), shape((2, own + TAIL, width), bf)),
+            out_shape=(shape((own, width), bf), shape((2, more, full), bf)),
             in_specs=[
                 flat(own, LANES), flat(TAIL, LANES), flat(GROW, LANES),
                 flat(own, LANES), flat(MEDIUM, LANES), flat(TAIL, LANES),
                 flat(own, LANES), flat(GROW, LANES),
-                cube(1, 8, LANES),
+                whole((1, 8, groups)),
                 pl.BlockSpec((8, MEDIUM), lambda i: (i, 0)),
                 pl.BlockSpec((8, MEDIUM), lambda i: (i, 0)),
                 whole(seg_col.shape), whole(seg_row.shape),
             ],
-            out_specs=(flat(own, LANES), cube(2, own + TAIL, LANES)),
+            out_specs=(flat(own, LANES), ANY),
             scratch_shapes=[
                 pltpu.VMEM((cols, LANES), f32),
                 pltpu.VMEM((SHORT - 1, grow, LANES), f32),
@@ -366,29 +401,23 @@
                 pltpu.VMEM((own + 2 * MEDIUM, LANES), bf),
                 pltpu.VMEM((own, LANES), f32),
                 pltpu.VMEM((grow, LANES), f32),
+                pltpu.VMEM((tiles, 2, own + TAIL, LANES), bf),
+                dma((tiles, chans)), dma((tiles, chans)), dma((tiles,)),
             ],
-            compiler_params=pltpu.CompilerParams(vmem_limit_bytes=40 << 20),
+            compiler_params=pltpu.CompilerParams(
+                collective_id=2, has_side_effects=True, vmem_limit_bytes=limit),
             name="mix_tile",
-        )(q, qprev, qnext, gown, gprev, gnext, cotangent, cnext, mytaps, filt, filt_rev, seg_col, seg_row)
-
-        back = pl.pallas_call(
-            functools.partial(third_kernel, chans, seqs),
-            out_shape=shape((2, more, full), bf),
-            in_specs=[ANY],
-            out_specs=ANY,
-            scratch_shapes=[dma((chans,)), dma((chans,)), dma],
-            compiler_params=pltpu.CompilerParams(collective_id=2, has_side_effects=True),
-            name="third_parts",
-        )(grads)
+        )(q, qprev, qnext, gown, gprev, gnext, cotangent, cnext, ctaps[:1], filt, filt_rev, seg_col, seg_row)
 
         grad = pl.pallas_call(
-            last_kernel,
-            grid=(full // WIDE,),
+            functools.partial(last_kernel, span),
+            grid=(full // wide,),
             out_shape=shape((3, rows, full), bf),
-            in_specs=[cube(2, more, WIDE), cube(2, more, WIDE), cube(3, 8, WIDE), whole(rseg_col.shape)],
-            out_specs=cube(3, rows, WIDE),
-            scratch_shapes=[pltpu.VMEM((SHORT - 1, more, LANES), f32), pltpu.VMEM((3, more, WIDE), f32)],
-            compiler_params=pltpu.CompilerParams(vmem_limit_bytes=40 << 20),
+            in_specs=[cube(2, more, wide), cube(2, more, wide), whole(taps.shape), whole(rseg_col.shape)],
+            out_specs=cube(3, rows, wide),
+            scratch_shapes=[pltpu.VMEM((SHORT - 1, more, LANES), f32), pltpu.VMEM((3, more, wide), f32),
+                            pltpu.VMEM((3, 8, wide), f32)],
+            compiler_params=pltpu.CompilerParams(vmem_limit_bytes=limit),
             name="last_rows",
         )(back, kv, taps, rseg_col)
         return hy, jnp.transpose(grad, (1, 0, 2))

time: 153 us -> 119 us (0.78)
  local copies, waits for them, and re-layouts: 36.1 us -> 5.89 us
  Pallas kernels: 114 us -> 108 us
    unnamed x38 -> x5, local copies, waits for them, and re-layouts: 20.8 us -> 0.98 us
    reshape x2 -> x0, local copies, waits for them, and re-layouts: 8.08 us -> none  [the longest x1 7.27 us: body(): jnp.repeat(jnp.transpose(taps, (1, 2, 0, 3)).reshape(3, 8, groups * chans...]
    pallas_call x4 -> x3, Pallas kernels: 61 us -> 55.6 us  [the longest x1 33.3 us: body(): pl.pallas_call(functools.partial(mix_kernel, chans, own, span), grid=(wid...]
    broadcast_in_dim x3 -> x0, local copies, waits for them, and re-layouts: 4.82 us -> none  [the longest x1 3.72 us: body(): jnp.repeat(jnp.transpose(taps, (1, 2, 0, 3)).reshape(3, 8, groups * chans...]
where the time goes in v3:
time: 119 us; the launch traced here: 117 us
  Pallas kernels  108 us (91%)
  local copies, waits for them, and re-layouts  5.89 us (5%)
  other arithmetic  2.43 us (2%)
    pallas_call x1, Pallas kernels, body(): pl.pallas_call(functools.partial(mix_kernel, chans, own, span), grid=(wid...  33.3 us
    pallas_call x1, Pallas kernels, body(): pl.pallas_call(functools.partial(second_kernel, chans, seqs), out_shape=t...  30.6 us
    pallas_call x1, Pallas kernels, body(): pl.pallas_call(functools.partial(first_kernel, chans, seqs), out_shape=(s...  22.1 us
    pallas_call x1, Pallas kernels, body(): pl.pallas_call(functools.partial(last_kernel, span), grid=(full // wide,)...  11.8 us
    pallas_call x1, Pallas kernels, body(): pl.pallas_call(functools.partial(gate_kernel, span), grid=(full // wide,)...  10.5 us

profile of v3, /device:TPU:0, one launch (start us, length us, event | category | flops | bytes accessed | tf_op | source)
XLA Modules:
  0.0 117.4 jit_solution(12759865478828088725)
XLA Ops:
  0.6 0.7 multiply_add_fusion
  1.3 0.1 convert_reduce_fusion.1
  1.4 1.3 %pad_slice_fusion.ctaps = f32[1,8,128]{2,1,0:T(8,128)} fusion(f32[3,7,128]{2,1,0:T(8,128)} %bitcast.8), kind=kLoop, calls=%fused_computation.10 | loop fusion | bytes 14848 | tf_op jit(solution)/shard_map/slice | solution.py:410
  2.7 0.1 convert_reduce_fusion
  2.8 0.1 slice.22
  2.9 1.3 %pad.4.ctaps = f32[3,8,128]{2,1,0:T(8,128)} pad(f32[3,7,128]{2,1,0:T(8,128)} %bitcast.9, f32[]{:T(128)} %constant.12.clone.1), padding=0_0x0_1x0_0 | pad | bytes 23044 | tf_op jit(solution)/shard_map/jit(_pad)/pad | solution.py:318
  4.2 0.6 broadcast_in_dim.42.seg_row
  4.8 0.7 broadcast_in_dim.38.seg_col
  5.5 0.8 convert_convert_fusion.filt
  6.3 0.0 copy-start.1
  6.3 0.1 slice.24
  6.4 0.1 slice.21
  6.5 0.7 pad_maximum_fusion.filt_rev
  7.2 0.8 broadcast_in_dim.41.seg_col
  8.0 22.1 %first_parts.1 = (bf16[256,2048]{1,0:T(8,128)(2,1)}, bf16[2,8,8192]{2,1,0:T(8,128)(2,1)}, bf16[2,8,8192]{2,1,0:T(8,128)(2,1)}, f32[4,3,8,128]{3,2,1,0:T(8,128)}, bf16[144,2048]{1,0:T(8,128)(2,1)}) custom-call(bf16[3,64,8192]{2,1,0:T(8,128)(2,1)} %bitcast.4, bf16[256,2048]{1,0:T(8,128)(2,1)} %cot.3, f32[3,8,128]{2,1,0:T(8,128)} %pad.4.ctaps), custom_call_target="tpu_custom_call" | custom-call | tf_op jit(solution)/shard_map/first_parts/pallas_call | solution.py:319
  30.1 10.5 %gate_rows.1 = (bf16[64,8192]{1,0:T(8,128)(2,1)}, f32[2,72,8192]{2,1,0:T(8,128)}) custom-call(bf16[3,64,8192]{2,1,0:T(8,128)(2,1)} %bitcast.5, bf16[2,8,8192]{2,1,0:T(8,128)(2,1)} %get-tuple-element.17.xprev, bf16[2,8,8192]{2,1,0:T(8,128)(2,1)} %get-tuple-element.18.xnext, f32[4,3,8,128]{3,2,1,0:T(8,128)} %get-tuple-element.19.ctaps, ...), custom_call_target="tpu_custom_call" | custom-call | tf_op jit(solution)/shard_map/gate_rows/pallas_call | solution.py:354
  40.6 0.0 copy-done.1
  40.6 30.6 %second_parts.1 = (bf16[256,2048]{1,0:T(8,128)(2,1)}, bf16[128,2048]{1,0:T(8,128)(2,1)}, bf16[16,2048]{1,0:T(8,128)(2,1)}, bf16[16,2048]{1,0:T(8,128)(2,1)}, bf16[144,2048]{1,0:T(8,128)(2,1)}) custom-call(bf16[256,2048]{1,0:T(8,128)(2,1)} %get-tuple-element.16.q, bf16[64,8192]{1,0:T(8,128)(2,1)} %get-tuple-element.20.gated), custom_call_target="tpu_custom_call" | custom-call | tf_op jit(solution)/shard_map/second_parts/pallas_call | solution.py:367
  71.3 33.3 %mix_tile.1 = (bf16[256,2048]{1,0:T(8,128)(2,1)}, bf16[2,72,8192]{2,1,0:T(8,128)(2,1)}) custom-call(bf16[256,2048]{1,0:T(8,128)(2,1)} %get-tuple-element.16.q, bf16[16,2048]{1,0:T(8,128)(2,1)} %get-tuple-element.21.qprev, bf16[144,2048]{1,0:T(8,128)(2,1)} %get-tuple-element.22.qnext, bf16[256,2048]{1,0:T(8,128)(2,1)} %get-tuple-element.23.gown, ...), custom_call_target="tpu_custom_call" | custom-call | tf_op jit(solution)/shard_map/mix_tile/pallas_call | solution.py:379
  104.6 0.0 copy-start
  104.6 11.8 %last_rows.1 = bf16[3,64,8192]{2,1,0:T(8,128)(2,1)} custom-call(bf16[2,72,8192]{2,1,0:T(8,128)(2,1)} %get-tuple-element.28.g, f32[2,72,8192]{2,1,0:T(8,128)} %get-tuple-element.29.kv, f32[4,3,8,128]{3,2,1,0:T(8,128)} %get-tuple-element.19.ctaps, s32[80,128]{1,0:T(8,128)} %broadcast_in_dim.38.seg_col), custom_call_target="tpu_custom_call" | custom-call | tf_op jit(solution)/shard_map/last_rows/pallas_call | solution.py:412
  116.4 0.0 copy-done
  116.4 1.0 copy.8
  (4 shorter events, 0.0 us)
Async XLA Ops:
  6.3 34.3 %copy-start.1 = (f32[128,128]{1,0:T(8,128)}, f32[128,128]{1,0:T(8,128)S(1)}, u32[]{:S(2)}) copy-start(f32[128,128]{1,0:T(8,128)S(1)} %convert_convert_fusion.filt) | copy-start | bytes 196612
  104.6 11.8 %copy-start = (bf16[256,2048]{1,0:T(8,128)(2,1)S(1)}, bf16[256,2048]{1,0:T(8,128)(2,1)}, u32[]{:S(2)}) copy-start(bf16[256,2048]{1,0:T(8,128)(2,1)} %get-tuple-element.32) | copy-start | bytes 3145732

commit v4 on v3

--- a/solution.py
+++ b/solution.py
@@ -51,66 +51,137 @@
     return pltpu.make_async_remote_copy(src, dst, ssem, rsem, device_id=dev, device_id_type=MESH)
 
 
-def first_kernel(chans, seqs, x, cot, ctaps, q, xprev, xnext, taps, cnext, ssem, rsem, tsem, usem, hs, hr, lsem):
+def front_kernel(chans, seqs, span, wide, x, cot, ctaps, seg_col, q, taps, cnext, gown, gprev, gnext, qprev, qnext, kv,
+                 xk, xprev, xnext, gated, kvv, fm, xs, tw, qs, qr, ts, tr, cs, cr, cl, hs, hr, ks, lsem):
     c, s = spot()
     rows = x.shape[1]
-    width = q.shape[1]
+    more = rows + EDGE
+    own, width = q.shape
+    per = width // wide
+    half = chans // 2
+    f32 = jnp.float32
     greet(chans, seqs, True, True)
     after, ahead = line_ends(chans, seqs)
-    copies = [
+    up, down = {"seq": lax.rem(s + 1, seqs)}, {"seq": lax.rem(s + seqs - 1, seqs)}
+    mine = pl.ds(pl.multiple_of(c * rows, 16), rows)
+    early = [
         remote(x.at[pl.ds(1, 2), pl.ds(rows - EDGE, EDGE)], xprev, hs.at[0], hr.at[0], after),
         remote(x.at[pl.ds(1, 2), pl.ds(0, EDGE)], xnext, hs.at[1], hr.at[1], ahead),
-        remote(cot.at[pl.ds(0, GROW)], cnext, hs.at[2], hr.at[2], {"seq": lax.rem(s + seqs - 1, seqs)}),
+        pltpu.make_async_copy(x.at[pl.ds(1, 2)], xk, lsem.at[0]),
+        pltpu.make_async_copy(ctaps, taps.at[c], lsem.at[1]),
     ]
+    queries = []
     for k in range(1, chans):
         d = lax.rem(c + k, chans)
-        copies.append(remote(ctaps, taps.at[c], tsem.at[k], usem.at[k], {"chan": d}))
-    place = q.at[pl.ds(pl.multiple_of(c * rows, 16), rows)]
-    for k in range(1, chans):
-        d = lax.rem(c + k, chans)
+        early.append(remote(ctaps, taps.at[c], ts.at[k], tr.at[k], {"chan": d}))
         part = x.at[0, :, pl.ds(pl.multiple_of(d * width, width), width)]
-        copies.append(remote(part, place, ssem.at[k], rsem.at[k], {"chan": d}))
-    mine = x.at[0, :, pl.ds(pl.multiple_of(c * width, width), width)]
-    copies.append(pltpu.make_async_copy(mine, place, lsem.at[0]))
-    copies.append(pltpu.make_async_copy(ctaps, taps.at[c], lsem.at[1]))
-    for cp in copies:
+        queries.append(remote(part, q.at[mine], qs.at[k], qr.at[k], {"chan": d}))
+    part = x.at[0, :, pl.ds(pl.multiple_of(c * width, width), width)]
+    qlocal = pltpu.make_async_copy(part, q.at[mine], lsem.at[2])
+    side = [remote(cot.at[pl.ds(0, GROW)], cnext, hs.at[2], hr.at[2], down)]
+    for cp in early + queries + [qlocal] + side:
         cp.start()
-    for cp in copies:
+    open_taps(fm, seg_col, EDGE, more)
+    for cp in early:
         cp.wait()
 
-
-def second_kernel(chans, seqs, q, gated, gown, gprev, gnext, qprev, qnext, ssem, rsem, hs, hr, lsem):
-    c, s = spot()
-    rows = gated.shape[0]
-    own, width = q.shape
-    greet(chans, seqs, True, False)
-    up, down = {"seq": lax.rem(s + 1, seqs)}, {"seq": lax.rem(s + seqs - 1, seqs)}
-    place = gown.at[pl.ds(pl.multiple_of(c * rows, 16), rows)]
-    main = []
-    for k in range(1, chans):
-        d = lax.rem(c + k, chans)
-        part = gated.at[:, pl.ds(pl.multiple_of(d * width, width), width)]
-        main.append(remote(part, place, ssem.at[k], rsem.at[k], {"chan": d}))
-    mine = gated.at[:, pl.ds(pl.multiple_of(c * width, width), width)]
-    local = pltpu.make_async_copy(mine, place, lsem)
-    side = [
-        remote(q.at[pl.ds(own - TAIL, TAIL)], qprev, hs.at[0], hr.at[0], up),
-        remote(q.at[pl.ds(0, GROW)], qnext, hs.at[1], hr.at[1], down),
+    def columns(n):
+        d = lax.rem(c + half + n // per, chans)
+        i = d * per + lax.rem(n, per)
+        return d, i, pl.ds(pl.multiple_of(i * wide, wide), wide)
+
+    def chunk_send(n):
+        k, p = n // per, lax.rem(n, per)
+        d, _, at = columns(n)
+        place = gown.at[mine, pl.ds(pl.multiple_of(p * wide, wide), wide)]
+        far = remote(gated.at[:, at], place, cs.at[n], cr.at[n], {"chan": d})
+        near = pltpu.make_async_copy(gated.at[:, at], place, cl.at[p])
+        return k == chans - half, far, near
+
+    def chunk_keep(n):
+        at = columns(n)[2]
+        return pltpu.make_async_copy(kvv.at[:, :, at], kv.at[:, :, at], ks.at[n])
+
+    def chunk(n, carry):
+        _, i, at = columns(n)
+        full = taps[i // per].reshape(24, taps.shape[3])
+        tw[...] = expand(full, lax.rem(i, per) * (wide // span), wide, span).reshape(3, 8, wide)
+        for m in range(2):
+            xs[m, pl.ds(0, EDGE), :] = xprev[m, :, at].astype(f32)
+            xs[m, pl.ds(EDGE, rows), :] = xk[m, :, at].astype(f32)
+            xs[m, pl.ds(EDGE + rows, EDGE), :] = xnext[m, :, at].astype(f32)
+        base = i * wide
+        for t in range(wide // LANES):
+            lane = pl.ds(t * LANES, LANES)
+            to = pl.ds(pl.multiple_of(base + t * LANES, LANES), LANES)
+            outs = []
+            for m in range(2):
+                total = tw[m + 1, 0:1, lane] * xs[m, pl.ds(EDGE, more), lane]
+                for j in range(1, SHORT):
+                    total = total + tw[m + 1, j : j + 1, lane] * (
+                        fm[j - 1] * xs[m, pl.ds(EDGE - j, more), lane])
+                kvv[m, :, to] = total
+                outs.append(total[:rows])
+            gated[:, to] = (outs[0] * outs[1]).astype(jnp.bfloat16)
+        home, far, near = chunk_send(n)
+
+        @pl.when(home)
+        def _():
+            near.start()
+
+        @pl.when(jnp.logical_not(home))
+        def _():
+            far.start()
+
+        chunk_keep(n).start()
+        return carry
+
+    lax.fori_loop(0, chans * per, chunk, 0)
+    for cp in queries:
+        cp.wait_recv()
+    qlocal.wait()
+    heads = [
+        remote(q.at[pl.ds(own - TAIL, TAIL)], qprev, hs.at[3], hr.at[3], up),
+        remote(q.at[pl.ds(0, GROW)], qnext, hs.at[4], hr.at[4], down),
     ]
-    for cp in main + [local] + side:
+    for cp in heads:
         cp.start()
-    for cp in main:
-        cp.wait_recv()
-    local.wait()
+
+    def arrive(n, carry):
+        home, far, near = chunk_send(n)
+
+        @pl.when(home)
+        def _():
+            near.wait()
+
+        @pl.when(jnp.logical_not(home))
+        def _():
+            far.wait_recv()
+
+        return carry
+
+    lax.fori_loop(0, chans * per, arrive, 0)
     late = [
-        remote(gown.at[pl.ds(own - MEDIUM, MEDIUM)], gprev, hs.at[2], hr.at[2], up),
-        remote(gown.at[pl.ds(0, TAIL)], gnext, hs.at[3], hr.at[3], down),
+        remote(gown.at[pl.ds(own - MEDIUM, MEDIUM)], gprev, hs.at[5], hr.at[5], up),
+        remote(gown.at[pl.ds(0, TAIL)], gnext, hs.at[6], hr.at[6], down),
     ]
     for cp in late:
         cp.start()
-    for cp in main:
+
+    def leave(n, carry):
+        home, far, _ = chunk_send(n)
+
+        @pl.when(jnp.logical_not(home))
+        def _():
+            far.wait_send()
+
+        chunk_keep(n).wait()
+        return carry
+
+    lax.fori_loop(0, chans * per, leave, 0)
+    for cp in queries:
         cp.wait_send()
-    for cp in side + late:
+    for cp in side + heads + late:
         cp.wait()
 
 
@@ -141,33 +212,6 @@
     for j in range(1, SHORT):
         same = seg_col[pl.ds(lo, n), :] == seg_col[pl.ds(lo - j, n), :]
         fm[j - 1, pl.ds(0, n), :] = jnp.where(same, 1.0, 0.0)
-
-
-def gate_kernel(span, x, xprev, xnext, ctaps, seg_col, gated, kv, fm, xs, taps):
-    spread(ctaps, taps, span)
-    rows = x.shape[1]
-    more = rows + EDGE
-
-    @pl.when(pl.program_id(0) == 0)
-    def _():
-        open_taps(fm, seg_col, EDGE, more)
-
-    f32 = jnp.float32
-    for m in range(2):
-        xs[m, pl.ds(0, EDGE), :] = xprev[m].astype(f32)
-        xs[m, pl.ds(EDGE, rows), :] = x[m + 1].astype(f32)
-        xs[m, pl.ds(EDGE + rows, EDGE), :] = xnext[m].astype(f32)
-    for t in range(x.shape[2] // LANES):
-        at = pl.ds(t * LANES, LANES)
-        outs = []
-        for m in range(2):
-            total = taps[m + 1, 0:1, at] * xs[m, pl.ds(EDGE, more), at]
-            for j in range(1, SHORT):
-                total = total + taps[m + 1, j : j + 1, at] * (
-                    fm[j - 1] * xs[m, pl.ds(EDGE - j, more), at])
-            kv[m, :, at] = total
-            outs.append(total[:rows])
-        gated[:, at] = (outs[0] * outs[1]).astype(jnp.bfloat16)
 
 
 def last_kernel(span, g, kv, ctaps, seg_col, out, fm, gs, taps):
@@ -316,17 +360,6 @@
         dma = pltpu.SemaphoreType.DMA
         x = jnp.transpose(features, (1, 0, 2))
         ctaps = jnp.pad(jnp.transpose(short_filter, (0, 2, 1)), ((0, 0), (0, 1), (0, 0)))
-        q, xprev, xnext, taps, cnext = pl.pallas_call(
-            functools.partial(first_kernel, chans, seqs),
-            out_shape=(
-                shape((own, width), bf), shape((2, EDGE, full), bf), shape((2, EDGE, full), bf),
-                shape((chans, 3, 8, groups), f32), shape((GROW, width), bf)),
-            in_specs=[ANY] * 3,
-            out_specs=(ANY,) * 5,
-            scratch_shapes=[dma((chans,))] * 4 + [dma((3,)), dma((3,)), dma((2,))],
-            compiler_params=pltpu.CompilerParams(collective_id=0, has_side_effects=True, vmem_limit_bytes=60 << 20),
-            name="first_parts",
-        )(x, cotangent, ctaps)
         wide = min(WIDE, width)
         limit = 60 << 20
 
@@ -351,28 +384,29 @@
         whole = lambda dims: pl.BlockSpec(dims, lambda i: (0,) * len(dims))
         flat = lambda n, w: pl.BlockSpec((n, w), lambda i: (0, i))
         cube = lambda m, n, w: pl.BlockSpec((m, n, w), lambda i: (0, 0, i))
-        gated, kv = pl.pallas_call(
-            functools.partial(gate_kernel, span),
-            grid=(full // wide,),
-            out_shape=(shape((rows, full), bf), shape((2, more, full), f32)),
-            in_specs=[cube(3, rows, wide), cube(2, EDGE, wide), cube(2, EDGE, wide), whole(taps.shape),
-                      whole(rseg_col.shape)],
-            out_specs=(flat(rows, wide), cube(2, more, wide)),
-            scratch_shapes=[pltpu.VMEM((SHORT - 1, more, LANES), f32),
-                            pltpu.VMEM((2, rows + 2 * EDGE, wide), f32), pltpu.VMEM((3, 8, wide), f32)],
-            compiler_params=pltpu.CompilerParams(vmem_limit_bytes=limit),
-            name="gate_rows",
-        )(x, xprev, xnext, taps, rseg_col)
-
-        gown, gprev, gnext, qprev, qnext = pl.pallas_call(
-            functools.partial(second_kernel, chans, seqs),
-            out_shape=tuple(shape((n, width), bf) for n in (own, MEDIUM, TAIL, TAIL, GROW)),
-            in_specs=[ANY] * 2,
-            out_specs=(ANY,) * 5,
-            scratch_shapes=[dma((chans,))] * 2 + [dma((4,)), dma((4,)), dma],
-            compiler_params=pltpu.CompilerParams(collective_id=1, has_side_effects=True, vmem_limit_bytes=limit),
-            name="second_parts",
-        )(q, gated)
+        pieces = chans * (width // wide)
+        vmem = pl.BlockSpec(memory_space=pltpu.VMEM)
+        parts = lambda n: shape((n, width), bf)
+        q, taps, cnext, gown, gprev, gnext, qprev, qnext, kv = pl.pallas_call(
+            functools.partial(front_kernel, chans, seqs, span, wide),
+            out_shape=(
+                parts(own), shape((chans, 3, 8, groups), f32), parts(GROW), parts(own), parts(MEDIUM), parts(TAIL),
+                parts(TAIL), parts(GROW), shape((2, more, full), f32)),
+            in_specs=[ANY, ANY, ANY, vmem],
+            out_specs=(ANY, vmem) + (ANY,) * 7,
+            scratch_shapes=[
+                pltpu.VMEM((2, rows, full), bf), pltpu.VMEM((2, EDGE, full), bf), pltpu.VMEM((2, EDGE, full), bf),
+                pltpu.VMEM((rows, full), bf), pltpu.VMEM((2, more, full), f32),
+                pltpu.VMEM((SHORT - 1, more, LANES), f32), pltpu.VMEM((2, rows + 2 * EDGE, wide), f32),
+                pltpu.VMEM((3, 8, wide), f32),
+                dma((chans,)), dma((chans,)), dma((chans,)), dma((chans,)),
+                dma((pieces,)), dma((pieces,)), dma((width // wide,)),
+                dma((7,)), dma((7,)), dma((pieces,)), dma((3,)),
+            ],
+            compiler_params=pltpu.CompilerParams(
+                collective_id=0, has_side_effects=True, vmem_limit_bytes=limit),
+            name="front",
+        )(x, cotangent, ctaps, rseg_col)
 
         blocks = own // MEDIUM
         tiles = width // LANES

time: 119 us -> 108 us (0.908)
  Pallas kernels: 108 us -> 97.4 us
    pallas_call x3 -> x1, Pallas kernels: 63.3 us -> 50.7 us  [body(): pl.pallas_call(functools.partial(front_kernel, chans, seqs, span, wide),...]
    pallas_call x1, Pallas kernels: 33.3 us -> 34.9 us  [body(): pl.pallas_call(functools.partial(mix_kernel, chans, own, span), grid=(wid...]
where the time goes in v4:
time: 108 us; the launch traced here: 106 us
  Pallas kernels  97.4 us (90%)
  local copies, waits for them, and re-layouts  5.9 us (5%)
  other arithmetic  2.42 us (2%)
    pallas_call x1, Pallas kernels, body(): pl.pallas_call(functools.partial(front_kernel, chans, seqs, span, wide),...  50.7 us
    pallas_call x1, Pallas kernels, body(): pl.pallas_call(functools.partial(mix_kernel, chans, own, span), grid=(wid...  34.9 us
    pallas_call x1, Pallas kernels, body(): pl.pallas_call(functools.partial(last_kernel, span), grid=(full // wide,)...  11.8 us

profile of v4, /device:TPU:0, one launch (start us, length us, event | category | flops | bytes accessed | tf_op | source)
XLA Modules:
  0.0 106.4 jit_solution(11216898507194362778)
XLA Ops:
  0.6 0.7 multiply_add_fusion
  1.3 0.1 convert_reduce_fusion.1
  1.4 1.3 %pad_slice_fusion.ctaps = f32[1,8,128]{2,1,0:T(8,128)} fusion(f32[3,7,128]{2,1,0:T(8,128)} %bitcast.7), kind=kLoop, calls=%fused_computation.10 | loop fusion | bytes 14848 | tf_op jit(solution)/shard_map/slice | solution.py:444
  2.7 0.1 convert_reduce_fusion
  2.8 0.1 slice.22
  2.9 1.3 %pad.4.ctaps = f32[3,8,128]{2,1,0:T(8,128)} pad(f32[3,7,128]{2,1,0:T(8,128)} %bitcast.8, f32[]{:T(128)} %constant.12.clone.1), padding=0_0x0_1x0_0 | pad | bytes 23044 | tf_op jit(solution)/shard_map/jit(_pad)/pad | solution.py:362
  4.2 0.6 broadcast_in_dim.42.seg_row
  4.8 0.7 broadcast_in_dim.38.seg_col
  5.5 0.8 convert_convert_fusion.filt
  6.3 0.0 copy-start.1
  6.3 0.1 slice.24
  6.4 0.1 slice.21
  6.5 0.7 pad_maximum_fusion.filt_rev
  7.2 0.8 broadcast_in_dim.41.seg_col
  8.0 50.7 %front.1 = (bf16[256,2048]{1,0:T(8,128)(2,1)}, f32[4,3,8,128]{3,2,1,0:T(8,128)}, bf16[144,2048]{1,0:T(8,128)(2,1)}, bf16[256,2048]{1,0:T(8,128)(2,1)}, bf16[128,...) custom-call(bf16[3,64,8192]{2,1,0:T(8,128)(2,1)} %bitcast.4, ...), custom_call_target="tpu_custom_call" | custom-call | tf_op jit(solution)/shard_map/front/pallas_call | solution.py:390
  58.7 0.0 copy-done.1
  58.7 34.9 %mix_tile.1 = (bf16[256,2048]{1,0:T(8,128)(2,1)}, bf16[2,72,8192]{2,1,0:T(8,128)(2,1)}) custom-call(bf16[256,2048]{1,0:T(8,128)(2,1)} %get-tuple-element.13.q, bf16[16,2048]{1,0:T(8,128)(2,1)} %get-tuple-element.14.qprev, bf16[144,2048]{1,0:T(8,128)(2,1)} %get-tuple-element.15.qnext, bf16[256,2048]{1,0:T(8,128)(2,1)} %get-tuple-element.16.gown, ...), custom_call_target="tpu_custom_call" | custom-call | tf_op jit(solution)/shard_map/mix_tile/pallas_call | solution.py:413
  93.7 0.0 copy-start
  93.7 11.8 %last_rows.1 = bf16[3,64,8192]{2,1,0:T(8,128)(2,1)} custom-call(bf16[2,72,8192]{2,1,0:T(8,128)(2,1)} %get-tuple-element.21.g, f32[2,72,8192]{2,1,0:T(8,128)} %get-tuple-element.22.kv, f32[4,3,8,128]{3,2,1,0:T(8,128)} %get-tuple-element.23.ctaps, s32[80,128]{1,0:T(8,128)} %broadcast_in_dim.38.seg_col), custom_call_target="tpu_custom_call" | custom-call | tf_op jit(solution)/shard_map/last_rows/pallas_call | solution.py:446
  105.5 0.0 copy-done
  105.5 1.0 copy.8
  (4 shorter events, 0.0 us)
Async XLA Ops:
  6.3 52.4 %copy-start.1 = (f32[128,128]{1,0:T(8,128)}, f32[128,128]{1,0:T(8,128)S(1)}, u32[]{:S(2)}) copy-start(f32[128,128]{1,0:T(8,128)S(1)} %convert_convert_fusion.filt) | copy-start | bytes 196612
  93.7 11.8 %copy-start = (bf16[256,2048]{1,0:T(8,128)(2,1)S(1)}, bf16[256,2048]{1,0:T(8,128)(2,1)}, u32[]{:S(2)}) copy-start(bf16[256,2048]{1,0:T(8,128)(2,1)} %get-tuple-element.26) | copy-start | bytes 3145732

commit v5 on v4

--- a/solution.py
+++ b/solution.py
@@ -79,19 +79,21 @@
     part = x.at[0, :, pl.ds(pl.multiple_of(c * width, width), width)]
     qlocal = pltpu.make_async_copy(part, q.at[mine], lsem.at[2])
     side = [remote(cot.at[pl.ds(0, GROW)], cnext, hs.at[2], hr.at[2], down)]
-    for cp in early + queries + [qlocal] + side:
+    for cp in early + side:
         cp.start()
     open_taps(fm, seg_col, EDGE, more)
     for cp in early:
         cp.wait()
+    for cp in queries + [qlocal]:
+        cp.start()
 
     def columns(n):
-        d = lax.rem(c + half + n // per, chans)
-        i = d * per + lax.rem(n, per)
+        d = lax.rem(c + half + lax.rem(n, chans), chans)
+        i = d * per + n // chans
         return d, i, pl.ds(pl.multiple_of(i * wide, wide), wide)
 
     def chunk_send(n):
-        k, p = n // per, lax.rem(n, per)
+        k, p = lax.rem(n, chans), n // chans
         d, _, at = columns(n)
         place = gown.at[mine, pl.ds(pl.multiple_of(p * wide, wide), wide)]
         far = remote(gated.at[:, at], place, cs.at[n], cr.at[n], {"chan": d})
@@ -160,13 +162,16 @@
 
         return carry
 
-    lax.fori_loop(0, chans * per, arrive, 0)
-    late = [
-        remote(gown.at[pl.ds(own - MEDIUM, MEDIUM)], gprev, hs.at[5], hr.at[5], up),
-        remote(gown.at[pl.ds(0, TAIL)], gnext, hs.at[6], hr.at[6], down),
-    ]
-    for cp in late:
-        cp.start()
+    late = []
+    for p in range(per):
+        lax.fori_loop(p * chans, (p + 1) * chans, arrive, 0)
+        at, e = pl.ds(p * wide, wide), 5 + 2 * p
+        late.append(remote(
+            gown.at[pl.ds(own - MEDIUM, MEDIUM), at], gprev.at[:, at], hs.at[e], hr.at[e], up))
+        late.append(remote(
+            gown.at[pl.ds(0, TAIL), at], gnext.at[:, at], hs.at[e + 1], hr.at[e + 1], down))
+        for cp in late[-2:]:
+            cp.start()
 
     def leave(n, carry):
         home, far, _ = chunk_send(n)
@@ -401,7 +406,7 @@
                 pltpu.VMEM((3, 8, wide), f32),
                 dma((chans,)), dma((chans,)), dma((chans,)), dma((chans,)),
                 dma((pieces,)), dma((pieces,)), dma((width // wide,)),
-                dma((7,)), dma((7,)), dma((pieces,)), dma((3,)),
+                dma((5 + 2 * (width // wide),)), dma((5 + 2 * (width // wide),)), dma((pieces,)), dma((3,)),
             ],
             compiler_params=pltpu.CompilerParams(
                 collective_id=0, has_side_effects=True, vmem_limit_bytes=limit),

time: 108 us -> 108 us (level)
    pallas_call x1, Pallas kernels: 50.7 us -> 52.2 us  [body(): pl.pallas_call(functools.partial(front_kernel, chans, seqs, span, wide),...]
where the time goes in v5:
time: 108 us; the launch traced here: 107 us
  Pallas kernels  97.9 us (91%)
  local copies, waits for them, and re-layouts  5.9 us (5%)
  other arithmetic  2.42 us (2%)
    pallas_call x1, Pallas kernels, body(): pl.pallas_call(functools.partial(front_kernel, chans, seqs, span, wide),...  52.2 us
    pallas_call x1, Pallas kernels, body(): pl.pallas_call(functools.partial(mix_kernel, chans, own, span), grid=(wid...  33.9 us
    pallas_call x1, Pallas kernels, body(): pl.pallas_call(functools.partial(last_kernel, span), grid=(full // wide,)...  11.8 us

profile of v5, /device:TPU:0, one launch (start us, length us, event | category | flops | bytes accessed | tf_op | source)
XLA Modules:
  0.0 106.9 jit_solution(15969537325589560343)
XLA Ops:
  0.6 0.7 multiply_add_fusion
  1.3 0.1 convert_reduce_fusion.1
  1.4 1.3 %pad_slice_fusion.ctaps = f32[1,8,128]{2,1,0:T(8,128)} fusion(f32[3,7,128]{2,1,0:T(8,128)} %bitcast.7), kind=kLoop, calls=%fused_computation.10 | loop fusion | bytes 14848 | tf_op jit(solution)/shard_map/slice | solution.py:449
  2.7 0.1 convert_reduce_fusion
  2.8 0.1 slice.22
  2.9 1.3 %pad.4.ctaps = f32[3,8,128]{2,1,0:T(8,128)} pad(f32[3,7,128]{2,1,0:T(8,128)} %bitcast.8, f32[]{:T(128)} %constant.12.clone.1), padding=0_0x0_1x0_0 | pad | bytes 23044 | tf_op jit(solution)/shard_map/jit(_pad)/pad | solution.py:367
  4.2 0.6 broadcast_in_dim.42.seg_row
  4.8 0.7 broadcast_in_dim.38.seg_col
  5.5 0.8 convert_convert_fusion.filt
  6.3 0.0 copy-start.1
  6.3 0.1 slice.24
  6.4 0.1 slice.21
  6.5 0.7 pad_maximum_fusion.filt_rev
  7.2 0.8 broadcast_in_dim.41.seg_col
  8.0 52.2 %front.1 = (bf16[256,2048]{1,0:T(8,128)(2,1)}, f32[4,3,8,128]{3,2,1,0:T(8,128)}, bf16[144,2048]{1,0:T(8,128)(2,1)}, bf16[256,2048]{1,0:T(8,128)(2,1)}, bf16[128,...) custom-call(bf16[3,64,8192]{2,1,0:T(8,128)(2,1)} %bitcast.4, ...), custom_call_target="tpu_custom_call" | custom-call | tf_op jit(solution)/shard_map/front/pallas_call | solution.py:395
  60.2 0.0 copy-done.1
  60.2 33.9 %mix_tile.1 = (bf16[256,2048]{1,0:T(8,128)(2,1)}, bf16[2,72,8192]{2,1,0:T(8,128)(2,1)}) custom-call(bf16[256,2048]{1,0:T(8,128)(2,1)} %get-tuple-element.13.q, bf16[16,2048]{1,0:T(8,128)(2,1)} %get-tuple-element.14.qprev, bf16[144,2048]{1,0:T(8,128)(2,1)} %get-tuple-element.15.qnext, bf16[256,2048]{1,0:T(8,128)(2,1)} %get-tuple-element.16.gown, ...), custom_call_target="tpu_custom_call" | custom-call | tf_op jit(solution)/shard_map/mix_tile/pallas_call | solution.py:418
  94.1 0.0 copy-start
  94.2 11.8 %last_rows.1 = bf16[3,64,8192]{2,1,0:T(8,128)(2,1)} custom-call(bf16[2,72,8192]{2,1,0:T(8,128)(2,1)} %get-tuple-element.21.g, f32[2,72,8192]{2,1,0:T(8,128)} %get-tuple-element.22.kv, f32[4,3,8,128]{3,2,1,0:T(8,128)} %get-tuple-element.23.ctaps, s32[80,128]{1,0:T(8,128)} %broadcast_in_dim.38.seg_col), custom_call_target="tpu_custom_call" | custom-call | tf_op jit(solution)/shard_map/last_rows/pallas_call | solution.py:451
  105.9 0.0 copy-done
  106.0 1.0 copy.8
  (4 shorter events, 0.0 us)
Async XLA Ops:
  6.3 53.9 %copy-start.1 = (f32[128,128]{1,0:T(8,128)}, f32[128,128]{1,0:T(8,128)S(1)}, u32[]{:S(2)}) copy-start(f32[128,128]{1,0:T(8,128)S(1)} %convert_convert_fusion.filt) | copy-start | bytes 196612
  94.1 11.8 %copy-start = (bf16[256,2048]{1,0:T(8,128)(2,1)S(1)}, bf16[256,2048]{1,0:T(8,128)(2,1)}, u32[]{:S(2)}) copy-start(bf16[256,2048]{1,0:T(8,128)(2,1)} %get-tuple-element.26) | copy-start | bytes 3145732
